TPU v7x, 128 devices: a whole 4x4x4 slice. The times are simulated.
128 devices in a mesh: blk: 32 (over z, x, y_lo), cols: 4 (over y_hi, core).
Axes of the slice: x: 4, y: 4 (y_hi: 2, y_lo: 2; y = y_hi * 2 + y_lo), z: 4, core: 2. Of those that a mesh axis runs over, the one named last changes fastest.
Arguments:
- focusing_plus: float32 [9728, 16, 512], P(('cols', 'blk')), may hold values from -6 to 6
- direct_field: float32 [9728, 16, 512], P(('cols', 'blk')), may hold values from -4 to 4
- reflectivity: float32 [2, 2, 9728, 9728], P(None, None, 'blk', 'cols'), may hold values from -0.0625 to 0.0625
- frequency_bins: int32 [2], replicated, may hold values from 64 to 247
- focal_onsets: int32 [16], replicated, may hold values from 32 to 191
- line_offsets: int32 [128], replicated, may hold values from 0 to 63
Outputs:
- focusing_update: float32 [9728, 16, 512], P(('cols', 'blk'))
All inputs are finite; a program needn't handle non-finite values.
Results may differ from a plain program's by a relative error of at most 0.000092.
Values sent between devices are 32-bit elements; how exact they have to be, the bound alone decides.
No kernel may reach another device: no remote copies, remote signals or barrier semaphores. Data moves between devices by JAX's collectives and lax.ppermute only.
A program may use at most 64 MiB of HBM per device.

v0:
```python
import math

import jax
import jax.numpy as jnp
from jax import lax
from jax.sharding import PartitionSpec as P

LINE = 76


highest = lax.Precision.HIGHEST


def wave_tables(frequency_bins, samples):
    times = jnp.arange(samples, dtype=jnp.int32)
    phases = frequency_bins[:, None] * times[None, :] % samples
    angles = phases.astype(jnp.float32) * (2.0 * math.pi / samples)
    inverse = jnp.stack([jnp.cos(angles), -jnp.sin(angles)], axis=1).reshape(-1, samples)
    forward = inverse / math.sqrt(samples)
    return (forward, inverse)


def to_spectrum(signal, forward):
    positions, focal, samples = signal.shape
    flat = signal.reshape(positions * focal, samples)
    result = lax.dot_general(
        forward,
        flat,
        (((1,), (1,)), ((), ())),
        precision=highest,
        preferred_element_type=jnp.float32,
    )
    return result.reshape(-1, 2, positions, focal)


def to_signal(spectrum, inverse):
    waves, halves, positions, focal = spectrum.shape
    flat = spectrum.reshape(waves * halves, positions * focal)
    result = lax.dot_general(
        flat,
        inverse,
        (((0,), (0,)), ((), ())),
        precision=highest,
        preferred_element_type=jnp.float32,
    )
    return result.reshape(positions, focal, -1)


def apply_window(signal, first_row, focal_onsets, line_offsets, line_length):
    positions, focal, samples = signal.shape
    lines = lax.dynamic_slice_in_dim(
        line_offsets, first_row // line_length, positions // line_length
    )
    per_row = jnp.repeat(lines, line_length)
    onsets = focal_onsets[None, :] + per_row[:, None]
    times = jnp.arange(samples, dtype=jnp.int32)
    window = (times[None, None, :] < onsets[:, :, None]) | (
        times[None, None, :] >= samples - onsets[:, :, None]
    )
    return jnp.where(window, signal, jnp.zeros_like(signal))


def kernel_apply(kernel, spectrum):
    parts = jnp.einsum("wprs,wqsf->wpqrf", kernel, spectrum, precision=highest)
    real = parts[:, 0, 0] - parts[:, 1, 1]
    imag = parts[:, 0, 1] + parts[:, 1, 0]
    return jnp.stack([real, imag], axis=1)


def adjoint_rows(kernel, spectrum):
    parts = jnp.einsum("wprs,wqrf->swpqf", kernel, spectrum, precision=highest)
    real = parts[:, :, 0, 0] + parts[:, :, 1, 1]
    imag = parts[:, :, 0, 1] - parts[:, :, 1, 0]
    stacked = jnp.stack([real, imag], axis=2)
    return stacked.reshape(stacked.shape[0], -1)


def local(focusing_plus, direct_field, reflectivity, frequency_bins, focal_onsets, line_offsets):
    samples = focusing_plus.shape[2]
    focal = focusing_plus.shape[1]
    waves = reflectivity.shape[0]
    block_rows = reflectivity.shape[2]
    group_columns = reflectivity.shape[3]
    own_sources = focusing_plus.shape[0]
    forward, inverse = wave_tables(frequency_bins, samples)
    own_spectrum = to_spectrum(focusing_plus, forward)
    gathered = lax.all_gather(own_spectrum, "blk", axis=2, tiled=True)
    partial_value = kernel_apply(reflectivity, gathered)
    block_index = lax.axis_index("blk")
    group_index = lax.axis_index("cols")
    share = lax.psum_scatter(partial_value, "cols", scatter_dimension=2, tiled=True)
    share_rows = share.shape[2]
    first_share = block_index * block_rows + group_index * share_rows
    minus_signal = apply_window(
        to_signal(share, inverse), first_share, focal_onsets, line_offsets, LINE
    )
    minus_rows = lax.all_gather(to_spectrum(minus_signal, forward), "cols", axis=2, tiled=True)
    summed = lax.psum_scatter(
        adjoint_rows(reflectivity, minus_rows), "blk", scatter_dimension=0, tiled=True
    )
    update = summed.reshape(own_sources, waves, 2, focal).transpose(1, 2, 0, 3)
    first_source = group_index * group_columns + block_index * own_sources
    correction = apply_window(
        to_signal(update, inverse), first_source, focal_onsets, line_offsets, LINE
    )
    return direct_field - correction


def solution(mesh):
    return jax.shard_map(
        local,
        mesh=mesh,
        in_specs=(
            P(("cols", "blk"), None, None),
            P(("cols", "blk"), None, None),
            P(None, None, "blk", "cols"),
            P(),
            P(),
            P(),
        ),
        out_specs=P(("cols", "blk"), None, None),
        check_vma=False,
    )
```

profile of v0, /device:TPU:0, one launch (start us, length us, event | category | flops | bytes accessed | tf_op | source)
XLA Modules:
  0.0 562.8 jit_solution(6611759334204949871)
XLA Ops:
  6.5 0.0 all-reduce.5.cloned.1.call-start
  6.5 0.9 fusion.40
  7.4 5.7 %fusion.10 = f32[2,2,76,16]{2,1,3,0:T(2,128)S(1)} fusion(f32[76,16,512]{2,1,0:T(8,128)} %param.6, f32[2,1,512]{2,1,0:T(1,128)S(1)} %get-tuple-element.14, f32[2,1,512]{2,1,0:T(1,128)S(1)} %get-tuple-element.13), kind=kOutput, calls=%fused_computation.8 | convolution fusion | flops 29888512 | bytes 2518016 | tf_op jit(solution)/shard_map/dot_general | solution.py:26
  13.1 0.2 copy.20
  13.2 137.0 %all_gather.6 = f32[2,2,2432,16]{3,1,0,2:T(2,128)S(1)} all-gather(f32[2,2,76,16]{3,1,0,2:T(2,128)S(1)} %copy.20), channel_id=1, replica_groups=mesh['blk'=32,'cols'=4] {'blk'}, dimensions={2}, use_global_device_ids=true | all-gather | bytes 642048 | tf_op jit(solution)/shard_map/all_gather | solution.py:87
  150.2 0.0 copy-start.1
  150.2 0.0 copy-start.2
  150.2 0.0 copy-start.4
  150.2 26.1 %fusion.17 = f32[2,2,2,304,16]{3,4,1,2,0:T(8,128)S(1)} fusion(f32[2,2,304,2432]{3,2,1,0:T(8,128)} %param.8, f32[2,2,2432,16,1]{3,1,0,2,4:T(2,128)S(1)} %bitcast.80), kind=kOutput, calls=%fused_computation.20 | convolution fusion | flops 1135607808 | bytes 12607488 | tf_op jit(solution)/shard_map/wprs,wqsf->wpqrf/dot_general | solution.py:64
  176.3 0.6 pad_maximum_fusion.1
  177.0 0.0 all-reduce.5.cloned.1.call-update
  177.0 0.3 all-reduce.7.cloned.1.call-start
  177.3 0.0 copy-done.1
  177.4 0.7 fusion.43
  178.0 0.0 copy-done.2
  178.0 1.3 broadcast_subtract_fusion
  179.3 0.0 copy-done.4
  179.3 0.6 dynamic-slice
  180.6 42.8 %all-reduce.5.cloned.1.call-done = f32[2,2,304,16]{2,3,0,1:T(8,128)} async-done(((f32[2,2,304,16]{2,3,0,1:T(8,128)}), f32[2,2,304,16]{2,3,0,1:T(8,128)}) %all-reduce.5.cloned.1.call-update) | async-done | bytes 77840
  223.3 0.9 constant_dynamic-slice_fusion.1
  224.3 0.1 copy.24
  224.4 0.1 reshape.229
  224.5 0.1 dot_general.29
  224.6 2.4 fusion.16
  227.1 4.0 fusion.8
  231.1 0.2 copy.27
  231.2 9.6 %all_gather.7 = f32[2,2,304,16]{3,1,0,2:T(2,128)S(1)} all-gather(f32[2,2,76,16]{3,1,0,2:T(2,128)S(1)} %copy.27), channel_id=1, replica_groups=mesh['blk'=32,'cols'=4] {'cols'}, dimensions={2}, use_global_device_ids=true | all-gather | bytes 97280 | tf_op jit(solution)/shard_map/all_gather | solution.py:97
  240.8 9.0 %fusion.5 = f32[2432,2,2,2,16]{0,4,2,3,1:T(8,128)S(1)} fusion(f32[2,2,304,2432]{3,2,1,0:T(8,128)} %param.8, f32[2,2,304,16,1]{3,1,0,2,4:T(2,128)S(1)} %bitcast.82), kind=kOutput, calls=%fused_computation.5 | convolution fusion | flops 1135607808 | bytes 13152256 | tf_op jit(solution)/shard_map/wprs,wqrf->swpqf/dot_general | solution.py:71
  249.9 0.0 copy-start.3
  249.9 0.0 copy-start
  250.0 0.9 copy.31
  250.9 0.0 all-reduce.7.cloned.1.call-update
  250.9 0.0 copy-done.3
  250.9 0.6 dynamic-slice.2
  252.0 298.5 %all-reduce.7.cloned.1.call-done = f32[2432,64]{0,1:T(8,128)} async-done(((f32[2432,64]{0,1:T(8,128)}), f32[2432,64]{0,1:T(8,128)}) %all-reduce.7.cloned.1.call-update) | async-done | bytes 622608
  550.5 0.9 constant_dynamic-slice_fusion
  551.4 0.1 copy.32
  551.6 0.1 reshape.233
  551.7 0.1 dot_general.34
  551.8 0.0 copy-done
  551.8 4.1 select_subtract_fusion
  (7 shorter events, 0.2 us)
Async XLA Ops:
  6.5 216.8 %all-reduce.5.cloned.1.call-start = ((), (), s32[]{:S(2)}) async-start(), calls=%async_computation | async-start | bytes 196608
  150.2 27.2 %copy-start.1 = (s32[128]{0:T(128)S(1)}, s32[128]{0:T(128)}, u32[]{:S(2)}) copy-start(s32[128]{0:T(128)} %param.11) | copy-start | bytes 1540
  150.2 27.8 %copy-start.2 = (s32[16]{0:T(128)S(1)}, s32[16]{0:T(128)}, u32[]{:S(2)}) copy-start(s32[16]{0:T(128)} %param.10) | copy-start | bytes 196
  150.2 29.1 %copy-start.4 = (u32[128]{0:T(128)S(1)}, u32[128]{0:T(128)}, u32[]{:S(2)}) copy-start(u32[128]{0:T(128)} %constant.57) | copy-start | bytes 1540
  177.0 373.5 %all-reduce.7.cloned.1.call-start = ((), (), s32[]{:S(2)}) async-start(), calls=%async_computation.1 | async-start | bytes 1245184
  249.9 1.1 copy-start.3
  249.9 301.9 %copy-start = (f32[76,16,512]{2,1,0:T(8,128)S(1)}, f32[76,16,512]{2,1,0:T(8,128)}, u32[]{:S(2)}) copy-start(f32[76,16,512]{2,1,0:T(8,128)} %param.7) | copy-start | bytes 7471108
Sparse Core Ops, SparseCore 0:
  177.1 46.1 all-reduce.4
  251.0 299.4 all-reduce.6
where the time goes:
time: 563 us
  waiting for transfers between devices  341 us (61%)
  blocking collectives  147 us (26%)
  matrix products  51.3 us (9%)
  between operations  14.8 us (3%)
  local copies, waits for them, and re-layouts  5.64 us (1%)
    unnamed x4, waiting for transfers between devices  341 us
    all_gather x1, blocking collectives, local(): gathered = lax.all_gather(own_spectrum, 'blk', axis=2, tiled=True)  137 us
    dot_general x1, matrix products, kernel_apply(): parts = jnp.einsum('wprs,wqsf->wpqrf', kernel, spectrum, precision=highest)  26.1 us
  transfers between devices with their start and end apart: 2, of which 2 were waited for; matrix products, arithmetic and copies ran while one was open for 1% of the time, Pallas kernels for 0%

commit v1 on v0

v1 whole, which is shorter than its diff:
```python
import math

import jax
import jax.numpy as jnp
from jax import lax
from jax.sharding import PartitionSpec as P

LINE = 76


highest = lax.Precision.HIGHEST
high = lax.Precision.HIGH


def wave_tables(frequency_bins, samples):
    times = jnp.arange(samples, dtype=jnp.int32)
    phases = frequency_bins[:, None] * times[None, :] % samples
    angles = phases.astype(jnp.float32) * (2.0 * math.pi / samples)
    inverse = jnp.stack([jnp.cos(angles), -jnp.sin(angles)], axis=1).reshape(-1, samples)
    forward = inverse / math.sqrt(samples)
    return (forward, inverse)


def windows(onsets, samples):
    times = jnp.arange(samples, dtype=jnp.int32)
    return (times < onsets[..., None]) | (times >= samples - onsets[..., None])


def local(focusing_plus, direct_field, reflectivity, frequency_bins, focal_onsets, line_offsets):
    own, focal, samples = focusing_plus.shape
    waves, _, block_rows, group_columns = reflectivity.shape
    parts = 2 * waves
    blocks = group_columns // own
    block_index = lax.axis_index("blk")
    group_index = lax.axis_index("cols")
    forward, inverse = wave_tables(frequency_bins, samples)

    spectrum = lax.dot_general(
        focusing_plus, forward, (((2,), (1,)), ((), ())), precision=high
    )
    spectrum = spectrum.transpose(0, 2, 1).reshape(own, parts * focal)
    width = parts * focal
    packed = spectrum.reshape(own * width // 128, 128)
    gathered = lax.all_to_all(
        jnp.broadcast_to(packed[None], (blocks,) + packed.shape), "blk", 0, 0
    )
    field = gathered.reshape(group_columns, waves, 2, focal)

    grown = jnp.einsum("wprs,swqf->wprqf", reflectivity, field, precision=high)
    real = grown[:, 0, :, 0] - grown[:, 1, :, 1]
    imag = grown[:, 0, :, 1] + grown[:, 1, :, 0]
    partial_value = jnp.stack([real, imag], axis=1)
    partial_value = partial_value.transpose(2, 0, 1, 3).reshape(-1, 128)
    shares = lax.all_gather(partial_value, "cols", axis=0)
    upgoing = shares.sum(0).reshape(block_rows // LINE, LINE, parts, focal)

    lines = lax.dynamic_slice_in_dim(line_offsets, block_index * (block_rows // LINE), block_rows // LINE)
    window = windows(lines[:, None] + focal_onsets[None, :], samples).astype(jnp.float32)
    pairs = (forward[:, None, :] * inverse[None, :, :]).reshape(parts * parts, samples)
    mixing = lax.dot_general(
        window.reshape(-1, samples), pairs, (((1,), (1,)), ((), ())), precision=highest
    ).reshape(block_rows // LINE, focal, parts, parts)
    minus = [
        sum(mixing[:, None, :, a, b] * upgoing[:, :, b] for b in range(parts))
        for a in range(parts)
    ]
    minus = jnp.stack(minus, axis=2).reshape(block_rows, waves, 2, focal)

    back = jnp.einsum("wprs,rwqf->swpqf", reflectivity, minus, precision=high)
    real = back[:, :, 0, 0] + back[:, :, 1, 1]
    imag = back[:, :, 0, 1] - back[:, :, 1, 0]
    adjoint = jnp.stack([real, imag], axis=2).reshape(blocks, own * width // 128, 128)
    scattered = lax.all_to_all(adjoint, "blk", 0, 0)
    update = scattered.sum(0).reshape(own, parts, focal)

    first_source = group_index * group_columns + block_index * own
    line = lax.dynamic_slice_in_dim(line_offsets, first_source // LINE, own // LINE)
    window = windows(jnp.repeat(line, LINE)[:, None] + focal_onsets[None, :], samples)
    signal = lax.dot_general(
        update, inverse, (((1,), (0,)), ((), ())), precision=high
    )
    return direct_field - jnp.where(window, signal, 0.0)


def solution(mesh):
    return jax.shard_map(
        local,
        mesh=mesh,
        in_specs=(
            P(("cols", "blk"), None, None),
            P(("cols", "blk"), None, None),
            P(None, None, "blk", "cols"),
            P(),
            P(),
            P(),
        ),
        out_specs=P(("cols", "blk"), None, None),
        check_vma=False,
    )
```

time: 563 us -> 129 us (0.23)
  waiting for transfers between devices: 341 us -> 25.3 us
  blocking collectives: 147 us -> 7.63 us
  local copies, waits for them, and re-layouts: 5.64 us -> 40.6 us
  matrix products: 51.3 us -> 33.9 us
  between operations: 14.8 us -> 0.27 us
  starting transfers between devices: 0.26 us -> 13.4 us
    unnamed x4 -> x0, waiting for transfers between devices: 341 us -> none
    all_gather x2 -> x1, blocking collectives: 147 us -> 7.63 us  [local(): shares = lax.all_gather(partial_value, 'cols', axis=0)]
    all_to_all x0 -> x2, waiting for transfers between devices: none -> 25.3 us  [the longest x1 13.2 us: local(): scattered = lax.all_to_all(adjoint, 'blk', 0, 0)]
    dot_general x6 -> x5, matrix products: 51.3 us -> 33.9 us  [the longest x1 20.6 us: local(): grown = jnp.einsum('wprs,swqf->wprqf', reflectivity, field, precision=high)]
    reshape x2 -> x5, local copies, waits for them, and re-layouts: 0.26 us -> 17 us  [the longest x1 8.46 us: local(): jnp.stack([real, imag], axis=2).reshape(blocks, own * width // 128, 128)]
    mul x0 -> x16, local copies, waits for them, and re-layouts: none -> 14.3 us  [local(): mixing[:, None, :, a, b] * upgoing[:, :, b]]
    all_to_all x0 -> x2, starting transfers between devices: none -> 13.4 us  [the longest x1 9.47 us: local(): lax.all_to_all(jnp.broadcast_to(packed[None], (blocks,) + packed.shape),...]
  transfers between devices with their start and end apart: 2 -> 2, of which waited for: 2 -> 2; matrix products, arithmetic and copies ran while one was open for 1% -> 2% of each run, Pallas kernels for 0% -> 0%
where the time goes in v1:
time: 129 us; the launch traced here: 128 us
  local copies, waits for them, and re-layouts  40.6 us (31%)
  matrix products  33.9 us (26%)
  waiting for transfers between devices  25.3 us (20%)
  starting transfers between devices  13.4 us (10%)
  blocking collectives  7.63 us (6%)
  other arithmetic  6.83 us (5%)
    dot_general x1, matrix products, local(): grown = jnp.einsum('wprs,swqf->wprqf', reflectivity, field, precision=high)  20.6 us
    mul x16, local copies, waits for them, and re-layouts, local(): mixing[:, None, :, a, b] * upgoing[:, :, b]  14.3 us
    all_to_all x1, waiting for transfers between devices, local(): scattered = lax.all_to_all(adjoint, 'blk', 0, 0)  13.2 us
    all_to_all x1, waiting for transfers between devices, local(): lax.all_to_all(jnp.broadcast_to(packed[None], (blocks,) + packed.shape),...  12.2 us
    all_to_all x1, starting transfers between devices, local(): lax.all_to_all(jnp.broadcast_to(packed[None], (blocks,) + packed.shape),...  9.47 us
    reshape x1, local copies, waits for them, and re-layouts, local(): jnp.stack([real, imag], axis=2).reshape(blocks, own * width // 128, 128)  8.46 us
    reshape x1, local copies, waits for them, and re-layouts, local(): field = gathered.reshape(group_columns, waves, 2, focal)  7.85 us
    all_gather x1, blocking collectives, local(): shares = lax.all_gather(partial_value, 'cols', axis=0)  7.63 us
  transfers between devices with their start and end apart: 2, of which 2 were waited for; matrix products, arithmetic and copies ran while one was open for 2% of the time, Pallas kernels for 0%

profile of v1, /device:TPU:0, one launch (start us, length us, event | category | flops | bytes accessed | tf_op | source)
XLA Modules:
  0.0 127.9 jit_solution(16348040170819696153)
XLA Ops:
  0.0 1.0 fusion.40
  1.1 0.6 copy-done.1
  1.6 0.1 copy-done
  1.7 2.5 %fusion.16 = f32[76,4,16]{0,1,2:T(4,128)S(1)} fusion(f32[76,16,512]{2,1,0:T(8,128)S(1)} %copy-done, f32[4,512]{1,0:T(4,128)S(1)} %reshape.301), kind=kOutput, calls=%fused_computation.13 | convolution fusion | flops 14944256 | bytes 2518016 | tf_op jit(solution)/shard_map/dot_general | solution.py:38
  4.2 0.1 copy.39
  4.4 0.1 broadcast_in_dim.7
  4.5 0.9 broadcast_in_dim.8
  5.4 9.5 %all-to-all-start = ((f32[32,38,128]{2,1,0:T(8,128)}), f32[32,38,128]{2,1,0:T(8,128)S(1)}, u32[]{:S(2)}, u32[]{:S(2)}) async-start(f32[32,38,128]{2,1,0:T(8,128)} %broadcast_in_dim.8), calls=%async_computation | async-start | bytes 1310720 | tf_op jit(solution)/shard_map/all_to_all | solution.py:44
  14.9 0.1 dynamic_slice.10
  15.1 0.5 fusion.24
  15.5 0.6 fusion.41
  16.2 12.2 %all-to-all-done = f32[32,38,128]{2,1,0:T(8,128)S(1)} async-done(((f32[32,38,128]{2,1,0:T(8,128)}), f32[32,38,128]{2,1,0:T(8,128)S(1)}, u32[]{:S(2)}, u32[]{:S(2)}) %all-to-all-start) | async-done | bytes 622624 | tf_op jit(solution)/shard_map/all_to_all | solution.py:44
  28.3 7.8 %reshape.302 = f32[2432,2,2,16]{3,2,1,0:T(2,128)} reshape(f32[32,38,128]{2,1,0:T(8,128)S(1)} %all-to-all-done) | data formatting | bytes 1245184 | tf_op jit(solution)/shard_map/reshape | solution.py:47
  36.2 20.6 %fusion.11 = f32[2,2,304,2,16]{2,4,1,3,0:T(8,128)S(1)} fusion(f32[2,2,304,2432]{3,2,1,0:T(8,128)} %param.8, f32[2432,2,2,16,1]{3,2,1,0,4:T(2,128)} %bitcast.83), kind=kOutput, calls=%fused_computation.12 | convolution fusion | flops 567803904 | bytes 12607488 | tf_op jit(solution)/shard_map/wprs,swqf->wprqf/dot_general | solution.py:49
  56.8 0.4 copy.43
  57.2 0.7 all_gather_reshape.3
  57.9 7.6 %all_gather.3 = f32[4,152,128]{2,1,0:T(8,128)S(1)} all-gather(f32[1,152,128]{2,1,0:T(8,128)S(1)} %all_gather_reshape.3), channel_id=1, replica_groups=mesh['blk'=32,'cols'=4] {'cols'}, dimensions={0}, use_global_device_ids=true | all-gather | bytes 389120 | tf_op jit(solution)/shard_map/all_gather | solution.py:54
  65.6 0.4 reshape.303
  66.0 1.6 %broadcast_multiply_fusion.15 = (f32[4,76,1,16]{3,2,1,0:T(1,128)}, f32[4,76,1,16]{3,2,1,0:T(1,128)}, f32[4,76,1,16]{3,2,1,0:T(1,128)}, f32[4,76,1,16]{3,2,1,0:T(...) fusion(f32[4,16]{1,0:T(4,128)S(1)} %bitcast.90, ...), kind=kLoop, calls=%fused_computation.44 | loop fusion | flops 34048 | bytes 196352 | tf_op jit(solution)/shard_map/mul | solution.py:64
  67.6 1.0 copy.44
  68.6 1.0 copy.58
  69.6 1.6 %copy.51 = f32[4,76,1,16]{1,3,2,0:T(8,128)} copy(f32[4,76,1,16]{3,2,1,0:T(1,128)} %get-tuple-element.18) | data formatting | bytes 38912 | tf_op jit(solution)/shard_map/mul | solution.py:64
  71.3 1.0 copy.55
  72.3 1.0 copy.59
  73.3 0.7 copy.47
  74.0 0.7 copy.46
  74.7 2.5 %broadcast_multiply_fusion.14 = (f32[4,76,1,16]{3,2,1,0:T(1,128)}, f32[4,76,1,16]{3,2,1,0:T(1,128)}, f32[4,76,1,16]{3,2,1,0:T(1,128)}, f32[4,76,1,16]{3,2,1,0:T(...) fusion(f32[4,16]{1,0:T(4,128)} %bitcast.91, ...), kind=kLoop, calls=%fused_computation.43 | loop fusion | flops 43776 | bytes 235776 | tf_op jit(solution)/shard_map/mul | solution.py:64
  77.2 1.0 copy.45
  78.2 1.0 copy.48
  79.2 1.0 copy.52
  80.2 1.0 copy.56
  81.2 1.0 copy.49
  82.2 1.0 copy.53
  83.2 1.0 copy.57
  84.2 0.1 copy.50
  84.3 0.1 copy.54
  84.5 0.8 add_add_fusion.2
  85.3 0.1 copy.60
  85.4 0.1 reshape.312
  85.5 6.4 %fusion.5 = f32[2432,2,2,2,16]{0,4,2,3,1:T(8,128)S(1)} fusion(f32[2,2,304,2432]{3,2,1,0:T(8,128)} %param.8, f32[304,2,2,16,1]{0,3,2,1,4:T(8,128)S(1)} %reshape.312), kind=kOutput, calls=%fused_computation.5 | convolution fusion | flops 567803904 | bytes 13152256 | tf_op jit(solution)/shard_map/wprs,rwqf->swpqf/dot_general | solution.py:69
  92.1 4.9 %copy.63 = f32[2432,2,2,16]{3,2,1,0:T(2,128)} copy(f32[2432,2,2,16]{0,3,1,2:T(8,128)S(1)} %pad_maximum_fusion) | data formatting | bytes 1245184 | tf_op jit(solution)/shard_map/stack | solution.py:72
  97.0 8.5 %reshape.305 = f32[32,38,128]{2,1,0:T(8,128)} reshape(f32[2432,2,2,16]{3,2,1,0:T(2,128)} %copy.63) | data formatting | bytes 1245184 | tf_op jit(solution)/shard_map/reshape | solution.py:72
  105.5 3.9 %all-to-all-start.1 = ((f32[32,38,128]{2,1,0:T(8,128)}), f32[32,38,128]{2,1,0:T(8,128)S(1)}, u32[]{:S(2)}, u32[]{:S(2)}) async-start(f32[32,38,128]{2,1,0:T(8,128)} %reshape.305), calls=%async_computation.1 | async-start | bytes 1310720 | tf_op jit(solution)/shard_map/all_to_all | solution.py:73
  109.4 0.6 dynamic_slice.8
  110.0 0.6 broadcast_subtract_fusion.1
  110.6 13.2 %all-to-all-done.1 = f32[32,38,128]{2,1,0:T(8,128)S(1)} async-done(((f32[32,38,128]{2,1,0:T(8,128)}), f32[32,38,128]{2,1,0:T(8,128)S(1)}, u32[]{:S(2)}, u32[]{:S(2)}) %all-to-all-start.1) | async-done | bytes 622624 | tf_op jit(solution)/shard_map/all_to_all | solution.py:73
  123.8 0.2 reshape.306
  124.0 3.9 %select_subtract_fusion = f32[76,16,512]{2,1,0:T(8,128)} fusion(f32[76,16,512]{2,1,0:T(8,128)} %param.7, f32[76,4,16]{2,1,0:T(4,128)S(1)} %reshape.306, f32[4,512,1]{1,0,2:T(4,128)S(1)} %reshape.313, s32[16]{0:T(128)S(1)} %get-tuple-element.5, s32[16]{0:T(128)S(1)} %get-tuple-element.6), kind=kOutput, calls=%fused_computation.8 | convolution fusion | flops 18055168 | bytes 5008512 | tf_op jit(solution)/shard_map/dot_general | solution.py:79
  (27 shorter events, 0.4 us)
Async XLA Ops:
  0.0 1.7 %copy-start = (f32[76,16,512]{2,1,0:T(8,128)S(1)}, f32[76,16,512]{2,1,0:T(8,128)}, u32[]{:S(2)}) copy-start(f32[76,16,512]{2,1,0:T(8,128)} %param.6) | copy-start | bytes 7471108
  1.0 0.6 copy-start.1
  1.7 13.2 %copy-start.5 = (s32[128]{0:T(128)S(1)}, s32[128]{0:T(128)}, u32[]{:S(2)}) copy-start(s32[128]{0:T(128)} %param.11) | copy-start | bytes 1540
  1.7 13.3 %copy-start.3 = (s32[16]{0:T(128)S(1)}, s32[16]{0:T(128)}, u32[]{:S(2)}) copy-start(s32[16]{0:T(128)} %param.10) | copy-start | bytes 196
  5.4 22.9 %all-to-all-start = ((f32[32,38,128]{2,1,0:T(8,128)}), f32[32,38,128]{2,1,0:T(8,128)S(1)}, u32[]{:S(2)}, u32[]{:S(2)}) async-start(f32[32,38,128]{2,1,0:T(8,128)} %broadcast_in_dim.8), calls=%async_computation | async-start | bytes 1310720 | tf_op jit(solution)/shard_map/all_to_all | solution.py:44
  97.0 12.4 %copy-start.2 = (f32[2,2,512]{2,1,0:T(2,128)S(1)}, f32[2,2,512]{2,1,0:T(2,128)}, u32[]{:S(2)}) copy-start(f32[2,2,512]{2,1,0:T(2,128)} %copy-done.1) | copy-start | bytes 24580
  97.0 12.4 %copy-start.6 = (s32[128]{0:T(128)S(1)}, s32[128]{0:T(128)}, u32[]{:S(2)}) copy-start(s32[128]{0:T(128)} %param.11) | copy-start | bytes 1540
  97.0 13.0 %copy-start.4 = (s32[16]{0:T(128)S(1)}, s32[16]{0:T(128)}, u32[]{:S(2)}) copy-start(s32[16]{0:T(128)} %param.10) | copy-start | bytes 196
  105.5 18.3 %all-to-all-start.1 = ((f32[32,38,128]{2,1,0:T(8,128)}), f32[32,38,128]{2,1,0:T(8,128)S(1)}, u32[]{:S(2)}, u32[]{:S(2)}) async-start(f32[32,38,128]{2,1,0:T(8,128)} %reshape.305), calls=%async_computation.1 | async-start | bytes 1310720 | tf_op jit(solution)/shard_map/all_to_all | solution.py:73

commit v2 on v1

v2 whole, which is shorter than its diff:
```python
import functools
import math

import jax
import jax.numpy as jnp
from jax import lax
from jax.experimental import pallas as pl
from jax.experimental.pallas import tpu as pltpu
from jax.sharding import PartitionSpec as P

LINE = 76
LANES = 128
HALF = 64
FOCAL = 16
PARTS = 4

VMEM = pl.BlockSpec(memory_space=pltpu.VMEM)
SMEM = pl.BlockSpec(memory_space=pltpu.SMEM)
ANY = pl.BlockSpec(memory_space=pl.ANY)
NT = (((1,), (1,)), ((), ()))
NN = (((1,), (0,)), ((), ()))
f32 = jnp.float32
bf16 = jnp.bfloat16


def dot(a, b, dims=NN, precision=None):
    return lax.dot_general(a, b, dims, precision=precision, preferred_element_type=f32)


def iota(shape, dim):
    return lax.broadcasted_iota(jnp.int32, shape, dim)


def rest_of(x):
    return x - x.astype(bf16).astype(f32)


def waves_of(bins, rows, samples, shift=0):
    shape = (rows, samples)
    part = (iota(shape, 0) + shift) & 3
    step = jnp.where(part < 2, bins[0], bins[1])
    phase = (step * iota(shape, 1) + (samples // 4) * (part & 1)) & (samples - 1)
    return jnp.cos(phase.astype(f32) * (2.0 * math.pi / samples))


def repeated(rows, times):
    one = jnp.concatenate(
        [jnp.broadcast_to(rows[k : k + 1], (FOCAL, rows.shape[1])) for k in range(PARTS)], 0
    )
    return jnp.concatenate([one] * times, 0) if times > 1 else one


def spectrum_kernel(
    chunks, bins_in, signal, kernel, out, early, bins, held, table, wide, sems, bins_sem, early_sem
):
    own, focal, samples = held.shape
    fetch = pltpu.make_async_copy(bins_in, bins, bins_sem)
    fetch.start()
    copies = []
    for i, (lo, hi) in enumerate(chunks):
        copies.append(
            pltpu.make_async_copy(signal.at[lo:hi], held.at[lo:hi], sems.at[i])
        )
        copies[-1].start()
    ahead = pltpu.make_async_copy(kernel.at[: early.shape[0]], early, early_sem)
    ahead.start()
    fetch.wait()
    forward = waves_of(bins, 8, samples) * (1.0 / math.sqrt(samples))
    table[0:HALF] = repeated(forward, 1).astype(bf16)
    table[HALF:LANES] = repeated(rest_of(forward), 1).astype(bf16)
    both = table[...]
    for (lo, hi), copy in zip(chunks, copies):
        copy.wait()
        x = held[lo:hi].reshape((hi - lo) * focal, samples)
        wide[lo * focal : hi * focal] = dot(x.astype(bf16), both, NT) + dot(
            rest_of(x).astype(bf16), both, NT
        )
    lane = iota((own, LANES), 1)
    total = jnp.zeros((own, LANES), f32)
    for f in range(focal):
        total = jnp.where((lane & 15) == f, wide[pl.ds(f, own, stride=focal), :], total)
    total = total + pltpu.roll(total, HALF, 1)
    half = own // 2
    packed = jnp.where(lane[:half] < HALF, total[:half], total[half:])
    out[...] = jnp.broadcast_to(packed[None], out.shape)
    ahead.wait()


def tables_kernel(axes, bins, focal_onsets, line_offsets, mixing, last):
    samples = last.shape[1]
    lines = mixing.shape[1]
    block = lax.axis_index(axes[0])
    group = lax.axis_index(axes[1])
    forward = waves_of(bins, 8, samples) * (1.0 / math.sqrt(samples))
    row = iota((FOCAL, samples), 0)
    time = iota((FOCAL, samples), 1)
    focal = jnp.zeros((FOCAL, samples), jnp.int32)
    for f in range(FOCAL):
        focal = jnp.where(row == f, focal_onsets[f], focal)

    def window(line):
        onset = focal + line_offsets[line]
        return jnp.where((time < onset) | (time >= samples - onset), 1.0, 0.0)

    shape = (lines * FOCAL, LANES)
    inside = jnp.concatenate([window(block * lines + l) for l in range(lines)], 0)
    same = (iota(shape, 0) & 15) == (iota(shape, 1) & 15)
    for d in range(PARTS):
        pair = repeated(forward * waves_of(bins, 8, samples, d), 2)
        value = jnp.where(same, dot(inside, pair, NT, lax.Precision.HIGHEST), 0.0)
        for l in range(lines):
            mixing[d, l : l + 1] = jnp.sum(
                value[l * FOCAL : (l + 1) * FOCAL], axis=0, keepdims=True
            )
    own = window(group * (line_offsets.shape[0] // 4) + block)
    inverse = repeated(waves_of(bins, 8, samples), 1) * jnp.concatenate([own] * PARTS, 0)
    high, low = inverse.astype(bf16), rest_of(inverse).astype(bf16)
    last[0:64] = high
    last[64:128] = high
    last[128:192] = low
    last[192:256] = low


def apply_kernel(chunks, field, early, kernel, out, high, low, late, rows, right, sems):
    first = early.shape[0]
    copies = {}
    for lo, hi in chunks:
        if lo >= first:
            copies[lo] = pltpu.make_async_copy(
                kernel.at[lo:hi], late.at[lo - first : hi - first], sems.at[len(copies)]
            )
            copies[lo].start()
    blocks, half, _ = field.shape
    lane = iota((half, LANES), 1)
    for b in range(blocks):
        x = field[b]
        turned = pltpu.roll(x, HALF, 1)
        rows[2 * half * b : 2 * half * b + half] = jnp.where(lane < HALF, x, turned)
        rows[2 * half * b + half : 2 * half * (b + 1)] = jnp.where(lane < HALF, turned, x)
    x = rows[...]
    right[...] = jnp.where(iota(x.shape, 1) < HALF, x, rest_of(x)).astype(bf16)
    count = high.shape[0] // PARTS
    terms = []
    for lo, hi in chunks:
        if lo < first:
            x = early[lo:hi]
        else:
            copies[lo].wait()
            x = late[lo - first : hi - first]
        upper, lower = x.astype(bf16), rest_of(x).astype(bf16)
        high[lo:hi] = upper
        low[lo:hi] = lower
        terms.append(dot(upper, right[...]) + dot(lower, right[...]))
    total = jnp.concatenate(terms, 0)
    lane = iota((count, LANES), 1)
    grown = []
    for w in range(2):
        parts = []
        for p in range(2):
            x = total[(2 * w + p) * count : (2 * w + p + 1) * count]
            parts.append(x + pltpu.roll(x, HALF, 1))
        real, imag = parts
        crossed = jnp.where(
            (lane & 16) == 0, -pltpu.roll(imag, LANES - 16, 1), pltpu.roll(imag, 16, 1)
        )
        grown.append(real + crossed)
    value = jnp.where((lane & 32) == 0, grown[0], grown[1])
    out[...] = jnp.where(lane[: count // 2] < HALF, value[: count // 2], value[count // 2 :])


def adjoint_kernel(one, other, mixing, high, low, out, flat, rows):
    count = high.shape[0] // PARTS
    x = one[...] + other[...]
    turned = pltpu.roll(x, HALF, 1)
    lane = iota(x.shape, 1)
    x = jnp.concatenate([jnp.where(lane < HALF, x, turned), jnp.where(lane < HALF, turned, x)], 0)
    row = iota(x.shape, 0)
    minus = jnp.zeros_like(x)
    for d in range(PARTS):
        weight = jnp.broadcast_to(mixing[d, 0:1], x.shape)
        for l in range(1, count // LINE):
            weight = jnp.where(row >= l * LINE, mixing[d, l : l + 1], weight)
        minus = minus + weight * (x if d == 0 else pltpu.roll(x, LANES - 16 * d, 1))
    minus = minus.T[:HALF]
    upper, lower = minus.astype(bf16), rest_of(minus).astype(bf16)
    for w in range(2):
        at = 32 * w
        total = None
        for p in range(2):
            if p == 0:
                left = [upper[at : at + 32], lower[at : at + 32]]
            else:
                left = []
                for v in (upper, lower):
                    left += [v[at + 16 : at + 32], -v[at : at + 16]]
            left = jnp.concatenate(left, 0)
            base = (2 * w + p) * count
            term = dot(left, high[base : base + count]) + dot(left, low[base : base + count])
            total = term if total is None else total + term
        flat[at : at + 32] = total[:32] + total[32:]
    columns = flat.shape[1]
    for j in range(columns // LANES):
        block = flat[:, j * LANES : (j + 1) * LANES]
        rows[j * LANES : (j + 1) * LANES] = jnp.concatenate([block, block], 0).T
    blocks, half, _ = out.shape
    lane = iota((half, LANES), 1)
    for b in range(blocks):
        at = 2 * half * b
        out[b] = jnp.where(lane < HALF, rows[at : at + half], rows[at + half : at + 2 * half])


def signal_kernel(chunks, pieces, last, direct, out, done, update, wide, out_sems):
    own, focal, samples = done.shape
    total = pieces[0]
    for b in range(1, pieces.shape[0]):
        total = total + pieces[b]
    turned = pltpu.roll(total, HALF, 1)
    half = own // 2
    lane = iota((half, LANES), 1)
    update[:half] = jnp.where(lane < HALF, total, turned)
    update[half:] = jnp.where(lane < HALF, turned, total)
    x = update[...]
    lane = iota(x.shape, 1)
    x = jnp.where(lane < HALF, x, rest_of(x))
    for f in range(focal):
        wide[pl.ds(f, own, stride=focal), :] = jnp.where((lane & 15) == f, x, 0.0)
    backs = []
    for i, (lo, hi) in enumerate(chunks):
        left = wide[lo * focal : hi * focal].astype(bf16)
        value = dot(jnp.concatenate([left, left], 1), last[...])
        done[lo:hi] = direct[lo:hi] - value.reshape(hi - lo, focal, samples)
        backs.append(pltpu.make_async_copy(done.at[lo:hi], out.at[lo:hi], out_sems.at[i]))
        backs[-1].start()
    for copy in backs:
        copy.wait()


def call(kernel, outs, ins, out_specs, scratch=(), cost=0, grid=None, limit=32):
    kwargs = {} if grid is None else dict(grid=grid)
    return pl.pallas_call(
        kernel,
        out_shape=outs,
        in_specs=ins,
        out_specs=out_specs,
        scratch_shapes=list(scratch),
        compiler_params=pltpu.CompilerParams(vmem_limit_bytes=limit << 20),
        cost_estimate=pl.CostEstimate(flops=cost, bytes_accessed=cost, transcendentals=0),
        **kwargs,
    )


def local(focusing_plus, direct_field, reflectivity, frequency_bins, focal_onsets, line_offsets):
    own, focal, samples = focusing_plus.shape
    waves, _, block_rows, columns = reflectivity.shape
    blocks = columns // own
    half = own // 2
    lines = block_rows // LINE
    assert (waves, focal, own) == (2, FOCAL, LINE)
    chunks = [(0, 16), (16, 40), (40, 64), (64, own)]
    shape = jax.ShapeDtypeStruct
    far = functools.partial(pltpu.with_memory_space_constraint, memory_space=pltpu.HBM)

    kernel = reflectivity.reshape(PARTS * block_rows, columns)
    first = 2 * block_rows
    copies, early = call(
        functools.partial(spectrum_kernel, chunks),
        [shape((blocks, half, LANES), f32), pltpu.VMEM((first, columns), f32)],
        [ANY, ANY, ANY],
        [VMEM, VMEM],
        [
            pltpu.SMEM(frequency_bins.shape, jnp.int32),
            pltpu.VMEM((own, focal, samples), f32),
            pltpu.VMEM((LANES, samples), bf16),
            pltpu.VMEM((own * focal, LANES), f32),
            pltpu.SemaphoreType.DMA((len(chunks),)),
            pltpu.SemaphoreType.DMA,
            pltpu.SemaphoreType.DMA,
        ],
        limit=24,
    )(far(frequency_bins), far(focusing_plus), far(kernel))
    field = lax.all_to_all(copies, "blk", 0, 0)

    mixing, last = call(
        functools.partial(tables_kernel, ("blk", "cols")),
        [shape((PARTS, lines, LANES), f32), shape((4 * HALF, samples), bf16)],
        [SMEM, SMEM, SMEM],
        [VMEM, VMEM],
        cost=1 << 20,
    )(frequency_bins, focal_onsets, line_offsets)

    cut = block_rows // 32 * 16
    pieces_of = [
        (p * block_rows + lo, p * block_rows + hi)
        for p in range(PARTS)
        for lo, hi in ((0, cut), (cut, block_rows))
    ]
    value, high, low = call(
        functools.partial(apply_kernel, pieces_of),
        [shape((block_rows // 2, LANES), f32)] + [pltpu.VMEM(kernel.shape, bf16)] * 2,
        [VMEM, VMEM, ANY],
        [VMEM] * 3,
        [
            pltpu.VMEM((kernel.shape[0] - first, columns), f32),
            pltpu.VMEM((columns, LANES), f32),
            pltpu.VMEM((columns, LANES), bf16),
            pltpu.SemaphoreType.DMA((len(pieces_of) // 2,)),
        ],
        limit=24,
    )(field, early, far(kernel))
    value = value + lax.ppermute(value, "cols", [(0, 1), (1, 0), (2, 3), (3, 2)])
    other = lax.ppermute(value, "cols", [(0, 2), (2, 0), (1, 3), (3, 1)])

    partial_update = call(
        adjoint_kernel,
        shape((blocks, half, LANES), f32),
        [VMEM] * 5,
        VMEM,
        [pltpu.VMEM((HALF, columns), f32), pltpu.VMEM((columns, LANES), f32)],
    )(value, other, mixing, high, low)
    pieces = lax.all_to_all(partial_update, "blk", 0, 0)

    return call(
        functools.partial(signal_kernel, chunks),
        shape((own, focal, samples), f32),
        [VMEM, VMEM, VMEM],
        ANY,
        [
            pltpu.VMEM((own, focal, samples), f32),
            pltpu.VMEM((own, LANES), f32),
            pltpu.VMEM((own * focal, LANES), f32),
            pltpu.SemaphoreType.DMA((len(chunks),)),
        ],
    )(pieces, last, direct_field)


def solution(mesh):
    return jax.shard_map(
        local,
        mesh=mesh,
        in_specs=(
            P(("cols", "blk"), None, None),
            P(("cols", "blk"), None, None),
            P(None, None, "blk", "cols"),
            P(),
            P(),
            P(),
        ),
        out_specs=P(("cols", "blk"), None, None),
        check_vma=False,
    )
```

time: 129 us -> 60.3 us (0.47)
  local copies, waits for them, and re-layouts: 40.6 us -> 0.01 us
  matrix products: 33.9 us -> 0 us
  blocking collectives: 7.63 us -> 39.4 us
  waiting for transfers between devices: 25.3 us -> 2.6 us
  Pallas kernels: 0 us -> 15 us
  starting transfers between devices: 13.4 us -> 3.07 us
  other arithmetic: 6.83 us -> 0.01 us
    all_to_all x0 -> x2, blocking collectives: none -> 39.4 us  [the longest x1 22.7 us: local(): field = lax.all_to_all(copies, 'blk', 0, 0)]
    dot_general x5 -> x0, matrix products: 33.9 us -> none  [the longest x1 20.6 us: local(): grown = jnp.einsum('wprs,swqf->wprqf', reflectivity, field, precision=high)]
    all_to_all x2 -> x0, waiting for transfers between devices: 25.3 us -> none  [the longest x1 13.2 us: local(): scattered = lax.all_to_all(adjoint, 'blk', 0, 0)]
    reshape x7 -> x0, local copies, waits for them, and re-layouts: 17 us -> none  [the longest x1 8.46 us: local(): jnp.stack([real, imag], axis=2).reshape(blocks, own * width // 128, 128)]
    pallas_call x0 -> x5, Pallas kernels: none -> 15 us  [the longest x1 4.96 us: local(): call(functools.partial(apply_kernel, pieces_of), [shape((block_rows // 2,...]
    mul x16 -> x0, local copies, waits for them, and re-layouts: 14.3 us -> none  [local(): mixing[:, None, :, a, b] * upgoing[:, :, b]]
    all_to_all x2 -> x0, starting transfers between devices: 13.4 us -> none  [the longest x1 9.47 us: local(): lax.all_to_all(jnp.broadcast_to(packed[None], (blocks,) + packed.shape),...]
    all_gather x1 -> x0, blocking collectives: 7.63 us -> none  [local(): shares = lax.all_gather(partial_value, 'cols', axis=0)]
  transfers between devices with their start and end apart: 2 -> 2, of which waited for: 2 -> 2; matrix products, arithmetic and copies ran while one was open for 2% -> 0% of each run, Pallas kernels for 0% -> 3%
where the time goes in v2:
time: 60.3 us; the launch traced here: 60.1 us
  blocking collectives  39.4 us (65%)
  Pallas kernels  15 us (25%)
  starting transfers between devices  3.07 us (5%)
  waiting for transfers between devices  2.6 us (4%)
    all_to_all x1, blocking collectives, local(): field = lax.all_to_all(copies, 'blk', 0, 0)  22.7 us
    all_to_all x1, blocking collectives, local(): pieces = lax.all_to_all(partial_update, 'blk', 0, 0)  16.6 us
    pallas_call x1, Pallas kernels, local(): call(functools.partial(apply_kernel, pieces_of), [shape((block_rows // 2,...  4.96 us
    pallas_call x1, Pallas kernels, local(): call(functools.partial(spectrum_kernel, chunks), [shape((blocks, half, LA...  3.51 us
    ppermute x1, starting transfers between devices, local(): other = lax.ppermute(value, 'cols', [(0, 2), (2, 0), (1, 3), (3, 1)])  2.98 us
    pallas_call x1, Pallas kernels, local(): call(adjoint_kernel, shape((blocks, half, LANES), f32), [VMEM] * 5, VMEM,...  2.92 us
    pallas_call x1, Pallas kernels, local(): call(functools.partial(signal_kernel, chunks), shape((own, focal, samples...  1.96 us
    pallas_call x1, Pallas kernels, local(): call(functools.partial(tables_kernel, ('blk', 'cols')), [shape((PARTS, li...  1.66 us
  transfers between devices with their start and end apart: 2, of which 2 were waited for; matrix products, arithmetic and copies ran while one was open for 0% of the time, Pallas kernels for 3%

profile of v2, /device:TPU:0, one launch (start us, length us, event | category | flops | bytes accessed | tf_op | source)
XLA Modules:
  0.0 60.1 jit_solution(18054937064410336983)
XLA Ops:
  0.0 3.5 %shard_map.64 = (f32[32,38,128]{2,1,0:T(8,128)S(1)}, f32[608,2432]{1,0:T(8,128)S(1)}) custom-call(s32[2]{0:T(128)} %bins.1, f32[76,16,512]{2,1,0:T(8,128)} %signal.1, f32[1216,2432]{1,0:T(8,128)} %bitcast.1), custom_call_target="tpu_custom_call" | custom-call | tf_op jit(solution)/shard_map/pallas_call | solution.py:265
  3.5 22.7 %all_to_all.10.field = f32[32,38,128]{2,1,0:T(8,128)S(1)} all-to-all(f32[32,38,128]{2,1,0:T(8,128)S(1)} %get-tuple-element.12), channel_id=1, replica_groups=mesh['blk'=32,'cols'=4] {'blk'}, dimensions={0} | all-to-all | bytes 1245184 | tf_op jit(solution)/shard_map/all_to_all | solution.py:281
  26.2 0.0 copy-start.1
  26.2 0.0 copy-start.2
  26.2 0.0 copy-start.3
  26.2 5.0 %shard_map.65 = (f32[152,128]{1,0:T(8,128)S(1)}, bf16[1216,2432]{1,0:T(8,128)(2,1)S(1)}, bf16[1216,2432]{1,0:T(8,128)(2,1)S(1)}) custom-call(f32[32,38,128]{2,1,0:T(8,128)S(1)} %all_to_all.10.field, f32[608,2432]{1,0:T(8,128)S(1)} %get-tuple-element.13.early, f32[1216,2432]{1,0:T(8,128)} %bitcast.2), custom_call_target="tpu_custom_call" | custom-call | tf_op jit(solution)/shard_map/pallas_call | solution.py:297
  31.2 0.1 collective-permute-start
  31.3 1.3 %collective-permute-done = f32[152,128]{1,0:T(8,128)S(1)} collective-permute-done((f32[152,128]{1,0:T(8,128)S(1)}, f32[152,128]{1,0:T(8,128)S(1)}, u32[]{:S(2)}, u32[]{:S(2)}) %collective-permute-start) | collective-permute-done | bytes 77856 | tf_op jit(solution)/shard_map/ppermute | solution.py:310
  32.6 3.0 %collective-permute-start.1 = (f32[152,128]{1,0:T(8,128)S(1)}, f32[152,128]{1,0:T(8,128)S(1)}, u32[]{:S(2)}, u32[]{:S(2)}) collective-permute-start(f32[152,128]{1,0:T(8,128)S(1)} %add.3.one), channel_id=1, source_target_pairs={{0,2},{2,0},{1,3},{3,1},{4,6},{6,4},{5,7},{7,5},{8,10},{10,8},{9,1... | collective-permute-start | bytes 233480 | tf_op jit(solution)/shard_map/ppermute | solution.py:311
  35.5 0.0 copy-done.1
  35.5 0.0 copy-done.2
  35.5 0.0 copy-done.3
  35.6 1.7 %shard_map.66 = (f32[4,4,128]{2,1,0:T(4,128)S(1)}, bf16[256,512]{1,0:T(8,128)(2,1)S(1)}) custom-call(s32[2]{0:T(128)S(1)} %copy-done.1, s32[16]{0:T(128)S(1)} %copy-done.2, s32[128]{0:T(128)S(1)} %copy-done.3), custom_call_target="tpu_custom_call" | custom-call | flops 1048576 | bytes 1048576 | tf_op jit(solution)/shard_map/pallas_call | solution.py:283
  37.2 1.3 %collective-permute-done.1.other = f32[152,128]{1,0:T(8,128)S(1)} collective-permute-done((f32[152,128]{1,0:T(8,128)S(1)}, f32[152,128]{1,0:T(8,128)S(1)}, u32[]{:S(2)}, u32[]{:S(2)}) %collective-permute-start.1) | collective-permute-done | bytes 77856 | tf_op jit(solution)/shard_map/ppermute | solution.py:311
  38.6 0.0 copy-start
  38.6 2.9 %shard_map.67 = f32[32,38,128]{2,1,0:T(8,128)S(1)} custom-call(f32[152,128]{1,0:T(8,128)S(1)} %add.3.one, f32[152,128]{1,0:T(8,128)S(1)} %collective-permute-done.1.other, f32[4,4,128]{2,1,0:T(4,128)S(1)} %get-tuple-element.15.mixing, bf16[1216,2432]{1,0:T(8,128)(2,1)S(1)} %get-tuple-element.16.high, bf16[1216,2432]{1,0:T(8,128)(2,1)S(1)} %get-tuple-element.17.low), custom_call_target="tpu_custom_call" | custom-call | tf_op jit(solution)/shard_map/pallas_call | solution.py:313
  41.5 16.6 %all_to_all.11.pieces = f32[32,38,128]{2,1,0:T(8,128)S(1)} all-to-all(f32[32,38,128]{2,1,0:T(8,128)S(1)} %shard_map.67), channel_id=1, replica_groups=mesh['blk'=32,'cols'=4] {'blk'}, dimensions={0} | all-to-all | bytes 1245184 | tf_op jit(solution)/shard_map/all_to_all | solution.py:320
  58.1 0.0 copy-done
  58.1 2.0 %shard_map.68 = f32[76,16,512]{2,1,0:T(8,128)} custom-call(f32[32,38,128]{2,1,0:T(8,128)S(1)} %all_to_all.11.pieces, bf16[256,512]{1,0:T(8,128)(2,1)S(1)} %get-tuple-element.18.last, f32[76,16,512]{2,1,0:T(8,128)S(1)} %copy-done), custom_call_target="tpu_custom_call" | custom-call | tf_op jit(solution)/shard_map/pallas_call | solution.py:322
  (1 shorter events, 0.0 us)
Async XLA Ops:
  26.2 9.3 %copy-start.1 = (s32[2]{0:T(128)S(1)}, s32[2]{0:T(128)}, u32[]{:S(2)}) copy-start(s32[2]{0:T(128)} %bins.1) | copy-start | bytes 28
  26.2 9.3 %copy-start.2 = (s32[16]{0:T(128)S(1)}, s32[16]{0:T(128)}, u32[]{:S(2)}) copy-start(s32[16]{0:T(128)} %focal_onsets.1) | copy-start | bytes 196
  26.2 9.3 %copy-start.3 = (s32[128]{0:T(128)S(1)}, s32[128]{0:T(128)}, u32[]{:S(2)}) copy-start(s32[128]{0:T(128)} %line_offsets.1) | copy-start | bytes 1540
  31.2 1.4 %collective-permute-start = (f32[152,128]{1,0:T(8,128)S(1)}, f32[152,128]{1,0:T(8,128)S(1)}, u32[]{:S(2)}, u32[]{:S(2)}) collective-permute-start(f32[152,128]{1,0:T(8,128)S(1)} %get-tuple-element.14), channel_id=1, source_target_pairs={{0,1},{1,0},{2,3},{3,2},{4,5},{5,4},{6,7},{7,6},{8,9},{9,8},{10,11... | collective-permute-start | bytes 233480 | tf_op jit(solution)/shard_map/ppermute | solution.py:310
  32.6 6.0 %collective-permute-start.1 = (f32[152,128]{1,0:T(8,128)S(1)}, f32[152,128]{1,0:T(8,128)S(1)}, u32[]{:S(2)}, u32[]{:S(2)}) collective-permute-start(f32[152,128]{1,0:T(8,128)S(1)} %add.3.one), channel_id=1, source_target_pairs={{0,2},{2,0},{1,3},{3,1},{4,6},{6,4},{5,7},{7,5},{8,10},{10,8},{9,1... | collective-permute-start | bytes 233480 | tf_op jit(solution)/shard_map/ppermute | solution.py:311
  38.6 19.6 %copy-start = (f32[76,16,512]{2,1,0:T(8,128)S(1)}, f32[76,16,512]{2,1,0:T(8,128)}, u32[]{:S(2)}) copy-start(f32[76,16,512]{2,1,0:T(8,128)} %direct.1) | copy-start | bytes 7471108

commit v3 on v2

v3 whole, which is shorter than its diff:
```python
import functools
import math

import jax
import jax.numpy as jnp
from jax import lax
from jax.experimental import pallas as pl
from jax.experimental.pallas import tpu as pltpu
from jax.sharding import PartitionSpec as P

LINE = 76
LANES = 128
HALF = 64
FOCAL = 16
PARTS = 4
SPAN = 512
DSPAN = 1280

VMEM = pl.BlockSpec(memory_space=pltpu.VMEM)
SMEM = pl.BlockSpec(memory_space=pltpu.SMEM)
ANY = pl.BlockSpec(memory_space=pl.ANY)
NT = (((1,), (1,)), ((), ()))
NN = (((1,), (0,)), ((), ()))
f32 = jnp.float32
bf16 = jnp.bfloat16


def dot(a, b, dims=NN, precision=None):
    return lax.dot_general(a, b, dims, precision=precision, preferred_element_type=f32)


def iota(shape, dim):
    return lax.broadcasted_iota(jnp.int32, shape, dim)


def rest_of(x):
    return x - x.astype(bf16).astype(f32)


def waves_of(bins, rows, samples, shift=0):
    shape = (rows, samples)
    part = (iota(shape, 0) + shift) & 3
    step = jnp.where(part < 2, bins[0], bins[1])
    phase = (step * iota(shape, 1) + (samples // 4) * (part & 1)) & (samples - 1)
    return jnp.cos(phase.astype(f32) * (2.0 * math.pi / samples))


def repeated(rows, times):
    one = jnp.concatenate(
        [jnp.broadcast_to(rows[k : k + 1], (FOCAL, rows.shape[1])) for k in range(PARTS)], 0
    )
    return jnp.concatenate([one] * times, 0) if times > 1 else one


def spectrum_kernel(chunks, bins_in, signal, wide, bins, held, table, sems, bins_sem):
    _, focal, samples = held.shape
    fetch = pltpu.make_async_copy(bins_in, bins, bins_sem)
    fetch.start()
    copies = []
    for i, (lo, hi) in enumerate(chunks):
        copies.append(
            pltpu.make_async_copy(signal.at[lo:hi], held.at[lo:hi], sems.at[i])
        )
        copies[-1].start()
    fetch.wait()
    forward = waves_of(bins, 8, samples) * (1.0 / math.sqrt(samples))
    table[0:HALF] = repeated(forward, 1).astype(bf16)
    table[HALF:LANES] = repeated(rest_of(forward), 1).astype(bf16)
    both = table[...]
    for (lo, hi), copy in zip(chunks, copies):
        copy.wait()
        x = held[lo:hi].reshape((hi - lo) * focal, samples)
        rounded = x.astype(bf16)
        wide[lo * focal : hi * focal] = dot(rounded, both, NT) + dot(
            (x - rounded.astype(f32)).astype(bf16), both, NT
        )


def pack_kernel(wide, _, out):
    own = 2 * out.shape[1]
    lane = iota((own, LANES), 1)
    total = jnp.zeros((own, LANES), f32)
    for f in range(FOCAL):
        total = jnp.where((lane & 15) == f, wide[pl.ds(f, own, stride=FOCAL), :], total)
    total = total + pltpu.roll(total, HALF, 1)
    half = own // 2
    packed = jnp.where(lane[:half] < HALF, total[:half], total[half:])
    out[...] = jnp.broadcast_to(packed[None], out.shape)


def tables_kernel(axes, bins, focal_onsets, line_offsets, mixing, last):
    samples = last.shape[1]
    lines = mixing.shape[2] // LINE
    block = lax.axis_index(axes[0])
    group = lax.axis_index(axes[1])
    forward = waves_of(bins, 8, samples) * (1.0 / math.sqrt(samples))
    row = iota((FOCAL, samples), 0)
    time = iota((FOCAL, samples), 1)
    focal = jnp.zeros((FOCAL, samples), jnp.int32)
    for f in range(FOCAL):
        focal = jnp.where(row == f, focal_onsets[f], focal)

    def window(line):
        onset = focal + line_offsets[line]
        return jnp.where((time < onset) | (time >= samples - onset), 1.0, 0.0)

    inside = jnp.concatenate([window(block * lines + l) for l in range(lines)], 0)
    rows = lines * FOCAL
    count = mixing.shape[2]
    same = (iota((HALF, rows), 0) & 15) == (iota((HALF, rows), 1) & 15)
    first = (iota((rows, count), 0) >> 4) * LINE
    column = iota((rows, count), 1)
    spread = jnp.where((column >= first) & (column < first + LINE), 1.0, 0.0)
    for d in range(PARTS):
        pair = repeated(forward * waves_of(bins, 8, samples, d), 1)
        value = jnp.where(same, dot(pair, inside, NT, lax.Precision.HIGHEST), 0.0)
        mixing[d] = dot(value, spread, NN, lax.Precision.HIGHEST)
    own = window(group * (line_offsets.shape[0] // 4) + block)
    inverse = repeated(waves_of(bins, 8, samples), 1) * jnp.concatenate([own] * PARTS, 0)
    high, low = inverse.astype(bf16), rest_of(inverse).astype(bf16)
    last[0:64] = high
    last[64:128] = high
    last[128:192] = low
    last[192:256] = low


def apply_kernel(order, field, kernel, out, high, low, rows, left, sums):
    blocks, half, _ = field.shape
    columns = left.shape[1]
    count = high.shape[0] // PARTS
    spans = [slice(lo, min(lo + SPAN, columns)) for lo in range(0, columns, SPAN)]
    units = [(span, k) for span in spans for k in range(PARTS)]
    ready = [0]

    def prepare(span):
        lane = iota((half, LANES), 1)
        while ready[0] * 2 * half < span.stop:
            b = ready[0]
            x = field[order.index(b)]
            turned = pltpu.roll(x, HALF, 1)
            rows[2 * half * b : 2 * half * b + half] = jnp.where(lane < HALF, x, turned)
            rows[2 * half * b + half : 2 * half * (b + 1)] = jnp.where(lane < HALF, turned, x)
            ready[0] += 1
        lane = iota((LANES, LANES), 1)
        for j in range(span.start, span.stop, LANES):
            x = rows[j : j + LANES]
            left[:, j : j + LANES] = jnp.where(lane < HALF, x, rest_of(x)).T.astype(bf16)

    def split(span, k):
        for c in range(0, count, 16):
            at = slice(k * count + c, k * count + c + 16)
            x = kernel[k // 2, k % 2, c : c + 16, span]
            high[at, span] = x.astype(bf16)
            x = x - high[at, span].astype(f32)
            low[at, span] = x.astype(bf16)

    split(*units[0])
    prepare(spans[0])
    for i, (span, k) in enumerate(units):
        at = slice(k * count, (k + 1) * count)
        w = 32 * (k // 2)
        upper = left[w : w + 32, span]
        both = jnp.concatenate([upper, left[HALF + w : HALF + w + 32, span]], 0)
        x = dot(both, high[at, span], NT)
        x = x[:32] + x[32:] + dot(upper, low[at, span], NT)
        sums[k] = x if span.start == 0 else sums[k] + x
        if i + 1 < len(units):
            split(*units[i + 1])
            if units[i + 1][0] is not span:
                prepare(units[i + 1][0])
    for w in range(2):
        real, imag = sums[2 * w], sums[2 * w + 1]
        out[32 * w : 32 * w + 16] = real[:16] - imag[16:]
        out[32 * w + 16 : 32 * w + 32] = real[16:] + imag[:16]


def adjoint_kernel(order, one, other, mixing, high, low, out, flat, rows):
    count = high.shape[0] // PARTS
    x = one[...] + other[...]
    minus = mixing[0] * x
    for d in range(1, PARTS):
        at = FOCAL * d
        minus = minus + mixing[d] * jnp.concatenate([x[at:], x[:at]], 0)
    upper, lower = minus.astype(bf16), rest_of(minus).astype(bf16)
    columns = flat.shape[1]
    lefts = []
    for w in range(2):
        at = 32 * w
        lefts.append(jnp.concatenate([upper[at : at + 32], lower[at : at + 32]], 0))
        left = []
        for v in (upper, lower):
            left += [v[at + 16 : at + 32], -v[at : at + 16]]
        lefts.append(jnp.concatenate(left, 0))
    for lo in range(0, columns, DSPAN):
        at = slice(lo, min(lo + DSPAN, columns))
        for w in range(2):
            total = None
            for p in range(2):
                left = lefts[2 * w + p]
                base = (2 * w + p) * count
                term = dot(left, high[base : base + count, at])
                term = term[:32] + term[32:] + dot(left[:32], low[base : base + count, at])
                total = term if total is None else total + term
            flat[32 * w : 32 * w + 32, at] = total
        for j in range(at.start, at.stop, LANES):
            block = flat[:, j : j + LANES]
            rows[j : j + LANES] = jnp.concatenate([block, block], 0).T
    blocks, half, _ = out.shape
    lane = iota((half, LANES), 1)
    for b in range(blocks):
        at = 2 * half * b
        out[order.index(b)] = jnp.where(lane < HALF, rows[at : at + half], rows[at + half : at + 2 * half])


def signal_kernel(chunks, pieces, last, direct, out, done, update, wide, out_sems):
    own, focal, samples = done.shape
    total = pieces[0]
    for b in range(1, pieces.shape[0]):
        total = total + pieces[b]
    turned = pltpu.roll(total, HALF, 1)
    half = own // 2
    lane = iota((half, LANES), 1)
    update[:half] = jnp.where(lane < HALF, total, turned)
    update[half:] = jnp.where(lane < HALF, turned, total)
    x = update[...]
    lane = iota(x.shape, 1)
    x = jnp.where(lane < HALF, x, rest_of(x))
    for f in range(focal):
        wide[pl.ds(f, own, stride=focal), :] = jnp.where((lane & 15) == f, x, 0.0)
    backs = []
    for i, (lo, hi) in enumerate(chunks):
        left = wide[lo * focal : hi * focal].astype(bf16)
        value = dot(jnp.concatenate([left, left], 1), last[...])
        done[lo:hi] = direct[lo:hi] - value.reshape(hi - lo, focal, samples)
        backs.append(pltpu.make_async_copy(done.at[lo:hi], out.at[lo:hi], out_sems.at[i]))
        backs[-1].start()
    for copy in backs:
        copy.wait()


def members():
    return [(9 * i) % 32 for i in range(32)]


def call(kernel, outs, ins, out_specs, scratch=(), cost=0, grid=None, limit=32):
    kwargs = {} if grid is None else dict(grid=grid)
    return pl.pallas_call(
        kernel,
        out_shape=outs,
        in_specs=ins,
        out_specs=out_specs,
        scratch_shapes=list(scratch),
        compiler_params=pltpu.CompilerParams(vmem_limit_bytes=limit << 20),
        cost_estimate=pl.CostEstimate(flops=cost, bytes_accessed=cost, transcendentals=0),
        **kwargs,
    )


def local(focusing_plus, direct_field, reflectivity, frequency_bins, focal_onsets, line_offsets):
    own, focal, samples = focusing_plus.shape
    waves, _, block_rows, columns = reflectivity.shape
    blocks = columns // own
    half = own // 2
    lines = block_rows // LINE
    assert (waves, focal, own) == (2, FOCAL, LINE)
    chunks = [(0, 16), (16, 40), (40, 64), (64, own)]
    early = [(0, 48), (48, own)]
    order = members()
    assert sorted(order) == list(range(blocks))
    exchange = functools.partial(
        lax.all_to_all,
        axis_name="blk",
        split_axis=0,
        concat_axis=0,
        tiled=True,
        axis_index_groups=[order],
    )
    shape = jax.ShapeDtypeStruct
    far = functools.partial(pltpu.with_memory_space_constraint, memory_space=pltpu.HBM)

    wide = call(
        functools.partial(spectrum_kernel, early),
        pltpu.VMEM((own * focal, LANES), f32),
        [ANY, ANY],
        VMEM,
        [
            pltpu.SMEM(frequency_bins.shape, jnp.int32),
            pltpu.VMEM((own, focal, samples), f32),
            pltpu.VMEM((LANES, samples), bf16),
            pltpu.SemaphoreType.DMA((len(early),)),
            pltpu.SemaphoreType.DMA,
        ],
        limit=16,
    )(far(frequency_bins), far(focusing_plus))
    copies = call(
        pack_kernel,
        shape((blocks, half, LANES), f32),
        [VMEM, ANY],
        VMEM,
        limit=16,
    )(wide, far(reflectivity))
    field = exchange(copies)

    mixing, last = call(
        functools.partial(tables_kernel, ("blk", "cols")),
        [shape((PARTS, HALF, block_rows), f32), shape((4 * HALF, samples), bf16)],
        [SMEM, SMEM, SMEM],
        [VMEM, VMEM],
        cost=1 << 20,
    )(frequency_bins, focal_onsets, line_offsets)

    value, high, low = call(
        functools.partial(apply_kernel, order),
        [shape((HALF, block_rows), f32)] + [pltpu.VMEM((PARTS * block_rows, columns), bf16)] * 2,
        [VMEM, VMEM],
        [VMEM] * 3,
        [
            pltpu.VMEM((columns, LANES), f32),
            pltpu.VMEM((LANES, columns), bf16),
            pltpu.VMEM((PARTS, 32, block_rows), f32),
        ],
        limit=16,
    )(field, reflectivity)
    value = value + lax.ppermute(value, "cols", [(0, 1), (1, 0), (2, 3), (3, 2)])
    other = lax.ppermute(value, "cols", [(0, 2), (2, 0), (1, 3), (3, 1)])

    partial_update = call(
        functools.partial(adjoint_kernel, order),
        shape((blocks, half, LANES), f32),
        [VMEM] * 5,
        VMEM,
        [pltpu.VMEM((HALF, columns), f32), pltpu.VMEM((columns, LANES), f32)],
    )(value, other, mixing, high, low)
    pieces = exchange(partial_update)

    return call(
        functools.partial(signal_kernel, chunks),
        shape((own, focal, samples), f32),
        [VMEM, VMEM, VMEM],
        ANY,
        [
            pltpu.VMEM((own, focal, samples), f32),
            pltpu.VMEM((own, LANES), f32),
            pltpu.VMEM((own * focal, LANES), f32),
            pltpu.SemaphoreType.DMA((len(chunks),)),
        ],
    )(pieces, last, direct_field)


def solution(mesh):
    return jax.shard_map(
        local,
        mesh=mesh,
        in_specs=(
            P(("cols", "blk"), None, None),
            P(("cols", "blk"), None, None),
            P(None, None, "blk", "cols"),
            P(),
            P(),
            P(),
        ),
        out_specs=P(("cols", "blk"), None, None),
        check_vma=False,
    )
```

time: 60.3 us -> 57.9 us (0.960)
  Pallas kernels: 15 us -> 13.8 us
  blocking collectives: 39.4 us -> 38.2 us
    pallas_call x4 -> x5, Pallas kernels: 13 us -> 11.8 us  [the longest x1 3.97 us: local(): call(functools.partial(apply_kernel, order), [shape((HALF, block_rows), f...]
    all_to_all x2, blocking collectives: 39.4 us -> 38.2 us  [the longest x1 21.4 us: local(): field = exchange(copies)]
  transfers between devices with their start and end apart: 2 -> 2, of which waited for: 2 -> 2; matrix products, arithmetic and copies ran while one was open for 0% -> 0% of each run, Pallas kernels for 3% -> 4%
where the time goes in v3:
time: 57.9 us; the launch traced here: 57.5 us
  blocking collectives  38.2 us (66%)
  Pallas kernels  13.8 us (24%)
  starting transfers between devices  3.06 us (5%)
  waiting for transfers between devices  2.33 us (4%)
    all_to_all x1, blocking collectives, local(): field = exchange(copies)  21.4 us
    all_to_all x1, blocking collectives, local(): pieces = exchange(partial_update)  16.8 us
    pallas_call x1, Pallas kernels, local(): call(functools.partial(apply_kernel, order), [shape((HALF, block_rows), f...  3.97 us
    ppermute x1, starting transfers between devices, local(): other = lax.ppermute(value, 'cols', [(0, 2), (2, 0), (1, 3), (3, 1)])  2.98 us
    pallas_call x1, Pallas kernels, local(): call(functools.partial(spectrum_kernel, early), pltpu.VMEM((own * focal,...  2.85 us
    pallas_call x1, Pallas kernels, local(): call(functools.partial(tables_kernel, ('blk', 'cols')), [shape((PARTS, HA...  2.4 us
    pallas_call x1, Pallas kernels, local(): call(functools.partial(adjoint_kernel, order), shape((blocks, half, LANES...  2.36 us
    pallas_call x1, Pallas kernels, local(): call(functools.partial(signal_kernel, chunks), shape((own, focal, samples...  1.98 us
  transfers between devices with their start and end apart: 2, of which 2 were waited for; matrix products, arithmetic and copies ran while one was open for 0% of the time, Pallas kernels for 4%

profile of v3, /device:TPU:0, one launch (start us, length us, event | category | flops | bytes accessed | tf_op | source)
XLA Modules:
  0.0 57.5 jit_solution(3029975257946639111)
XLA Ops:
  0.0 2.8 %shard_map.64.wide = f32[1216,128]{1,0:T(8,128)S(1)} custom-call(s32[2]{0:T(128)} %bins.1, f32[76,16,512]{2,1,0:T(8,128)} %signal.1), custom_call_target="tpu_custom_call" | custom-call | tf_op jit(solution)/shard_map/pallas_call | solution.py:281
  2.9 0.0 copy-start
  2.9 0.2 shard_map.65
  3.1 21.4 %all_to_all.10.field = f32[32,38,128]{2,1,0:T(8,128)S(1)} all-to-all(f32[32,38,128]{2,1,0:T(8,128)S(1)} %shard_map.65), channel_id=1, replica_groups={{0,36,72,108,16,52,88,124,32,68,104,12,48,84,120,28,64,100,8,44,80,116,..., dimensions={0} | all-to-all | bytes 1245184 | tf_op jit(solution)/shard_map/all_to_all | solution.py:302
  24.5 0.0 copy-done
  24.5 0.0 copy-start.2
  24.5 0.0 copy-start.3
  24.5 0.0 copy-start.4
  24.5 4.0 %shard_map.66 = (f32[64,304]{1,0:T(8,128)S(1)}, bf16[1216,2432]{1,0:T(8,128)(2,1)S(1)}, bf16[1216,2432]{1,0:T(8,128)(2,1)S(1)}) custom-call(f32[32,38,128]{2,1,0:T(8,128)S(1)} %all_to_all.10.field, f32[2,2,304,2432]{3,2,1,0:T(8,128)S(1)} %copy-done), custom_call_target="tpu_custom_call" | custom-call | tf_op jit(solution)/shard_map/pallas_call | solution.py:312
  28.5 0.1 collective-permute-start
  28.6 1.3 %collective-permute-done = f32[64,304]{1,0:T(8,128)S(1)} collective-permute-done((f32[64,304]{1,0:T(8,128)S(1)}, f32[64,304]{1,0:T(8,128)S(1)}, u32[]{:S(2)}, u32[]{:S(2)}) %collective-permute-start) | collective-permute-done | bytes 77856 | tf_op jit(solution)/shard_map/ppermute | solution.py:324
  29.9 3.0 %collective-permute-start.1 = (f32[64,304]{1,0:T(8,128)S(1)}, f32[64,304]{1,0:T(8,128)S(1)}, u32[]{:S(2)}, u32[]{:S(2)}) collective-permute-start(f32[64,304]{1,0:T(8,128)S(1)} %add.3.one), channel_id=1, source_target_pairs={{0,2},{2,0},{1,3},{3,1},{4,6},{6,4},{5,7},{7,5},{8,10},{10,8},{9,1... | collective-permute-start | bytes 233480 | tf_op jit(solution)/shard_map/ppermute | solution.py:325
  32.9 0.0 copy-done.2
  32.9 0.0 copy-done.3
  32.9 0.0 copy-done.4
  32.9 2.4 %shard_map.67 = (f32[4,64,304]{2,1,0:T(8,128)S(1)}, bf16[256,512]{1,0:T(8,128)(2,1)S(1)}) custom-call(s32[2]{0:T(128)S(1)} %copy-done.2, s32[16]{0:T(128)S(1)} %copy-done.3, s32[128]{0:T(128)S(1)} %copy-done.4), custom_call_target="tpu_custom_call" | custom-call | flops 1048576 | bytes 1048576 | tf_op jit(solution)/shard_map/pallas_call | solution.py:304
  35.3 1.0 %collective-permute-done.1.other = f32[64,304]{1,0:T(8,128)S(1)} collective-permute-done((f32[64,304]{1,0:T(8,128)S(1)}, f32[64,304]{1,0:T(8,128)S(1)}, u32[]{:S(2)}, u32[]{:S(2)}) %collective-permute-start.1) | collective-permute-done | bytes 77856 | tf_op jit(solution)/shard_map/ppermute | solution.py:325
  36.3 0.0 copy-start.1
  36.3 2.4 %shard_map.68 = f32[32,38,128]{2,1,0:T(8,128)S(1)} custom-call(f32[64,304]{1,0:T(8,128)S(1)} %add.3.one, f32[64,304]{1,0:T(8,128)S(1)} %collective-permute-done.1.other, f32[4,64,304]{2,1,0:T(8,128)S(1)} %get-tuple-element.11.mixing, bf16[1216,2432]{1,0:T(8,128)(2,1)S(1)} %get-tuple-element.12.high, bf16[1216,2432]{1,0:T(8,128)(2,1)S(1)} %get-tuple-element.13.low), custom_call_target="tpu_custom_call" | custom-call | tf_op jit(solution)/shard_map/pallas_call | solution.py:327
  38.7 16.8 %all_to_all.11.pieces = f32[32,38,128]{2,1,0:T(8,128)S(1)} all-to-all(f32[32,38,128]{2,1,0:T(8,128)S(1)} %shard_map.68), channel_id=1, replica_groups={{0,36,72,108,16,52,88,124,32,68,104,12,48,84,120,28,64,100,8,44,80,116,..., dimensions={0} | all-to-all | bytes 1245184 | tf_op jit(solution)/shard_map/all_to_all | solution.py:334
  55.5 0.0 copy-done.1
  55.5 2.0 %shard_map.69 = f32[76,16,512]{2,1,0:T(8,128)} custom-call(f32[32,38,128]{2,1,0:T(8,128)S(1)} %all_to_all.11.pieces, bf16[256,512]{1,0:T(8,128)(2,1)S(1)} %get-tuple-element.14.last, f32[76,16,512]{2,1,0:T(8,128)S(1)} %copy-done.1), custom_call_target="tpu_custom_call" | custom-call | tf_op jit(solution)/shard_map/pallas_call | solution.py:336
  (1 shorter events, 0.0 us)
Async XLA Ops:
  2.9 21.7 %copy-start = (f32[2,2,304,2432]{3,2,1,0:T(8,128)S(1)}, f32[2,2,304,2432]{3,2,1,0:T(8,128)}, u32[]{:S(2)}) copy-start(f32[2,2,304,2432]{3,2,1,0:T(8,128)} %kernel.1) | copy-start | bytes 35487748
  24.5 8.4 %copy-start.2 = (s32[2]{0:T(128)S(1)}, s32[2]{0:T(128)}, u32[]{:S(2)}) copy-start(s32[2]{0:T(128)} %bins.1) | copy-start | bytes 28
  24.5 8.4 %copy-start.3 = (s32[16]{0:T(128)S(1)}, s32[16]{0:T(128)}, u32[]{:S(2)}) copy-start(s32[16]{0:T(128)} %focal_onsets.1) | copy-start | bytes 196
  24.5 8.4 %copy-start.4 = (s32[128]{0:T(128)S(1)}, s32[128]{0:T(128)}, u32[]{:S(2)}) copy-start(s32[128]{0:T(128)} %line_offsets.1) | copy-start | bytes 1540
  28.5 1.4 %collective-permute-start = (f32[64,304]{1,0:T(8,128)S(1)}, f32[64,304]{1,0:T(8,128)S(1)}, u32[]{:S(2)}, u32[]{:S(2)}) collective-permute-start(f32[64,304]{1,0:T(8,128)S(1)} %get-tuple-element.10), channel_id=1, source_target_pairs={{0,1},{1,0},{2,3},{3,2},{4,5},{5,4},{6,7},{7,6},{8,9},{9,8},{10,11... | collective-permute-start | bytes 233480 | tf_op jit(solution)/shard_map/ppermute | solution.py:324
  29.9 6.4 %collective-permute-start.1 = (f32[64,304]{1,0:T(8,128)S(1)}, f32[64,304]{1,0:T(8,128)S(1)}, u32[]{:S(2)}, u32[]{:S(2)}) collective-permute-start(f32[64,304]{1,0:T(8,128)S(1)} %add.3.one), channel_id=1, source_target_pairs={{0,2},{2,0},{1,3},{3,1},{4,6},{6,4},{5,7},{7,5},{8,10},{10,8},{9,1... | collective-permute-start | bytes 233480 | tf_op jit(solution)/shard_map/ppermute | solution.py:325
  36.3 19.2 %copy-start.1 = (f32[76,16,512]{2,1,0:T(8,128)S(1)}, f32[76,16,512]{2,1,0:T(8,128)}, u32[]{:S(2)}) copy-start(f32[76,16,512]{2,1,0:T(8,128)} %direct.1) | copy-start | bytes 7471108

commit v4 on v3

--- a/solution.py
+++ b/solution.py
@@ -52,28 +52,71 @@
     return jnp.concatenate([one] * times, 0) if times > 1 else one
 
 
-def spectrum_kernel(chunks, bins_in, signal, wide, bins, held, table, sems, bins_sem):
-    _, focal, samples = held.shape
-    fetch = pltpu.make_async_copy(bins_in, bins, bins_sem)
-    fetch.start()
-    copies = []
-    for i, (lo, hi) in enumerate(chunks):
-        copies.append(
-            pltpu.make_async_copy(signal.at[lo:hi], held.at[lo:hi], sems.at[i])
+def fill_tables(axes, waves, bins, focal_onsets, line_offsets, mixing, last):
+    samples = last.shape[1]
+    lines = mixing.shape[2] // LINE
+    block = lax.axis_index(axes[0])
+    group = lax.axis_index(axes[1])
+    row = iota((FOCAL, samples), 0)
+    time = iota((FOCAL, samples), 1)
+    focal = jnp.zeros((FOCAL, samples), jnp.int32)
+    for f in range(FOCAL):
+        focal = jnp.where(row == f, focal_onsets[f], focal)
+
+    def window(line):
+        onset = focal + line_offsets[line]
+        return jnp.where((time < onset) | (time >= samples - onset), 1.0, 0.0)
+
+    inside = jnp.concatenate([window(block * lines + l) for l in range(lines)], 0).astype(bf16)
+    rows = lines * FOCAL
+    count = mixing.shape[2]
+    same = (iota((HALF, rows), 0) & 15) == (iota((HALF, rows), 1) & 15)
+    first = (iota((rows, count), 0) >> 4) * LINE
+    column = iota((rows, count), 1)
+    spread = jnp.where((column >= first) & (column < first + LINE), 1.0, 0.0).astype(bf16)
+    forward = waves * (1.0 / math.sqrt(samples))
+    for d in range(PARTS):
+        pair = forward * waves_of(bins, 8, samples, d)
+        value = dot(repeated(pair, 1).astype(bf16), inside, NT) + dot(
+            repeated(rest_of(pair), 1).astype(bf16), inside, NT
         )
-        copies[-1].start()
-    fetch.wait()
-    forward = waves_of(bins, 8, samples) * (1.0 / math.sqrt(samples))
-    table[0:HALF] = repeated(forward, 1).astype(bf16)
-    table[HALF:LANES] = repeated(rest_of(forward), 1).astype(bf16)
+        value = jnp.where(same, value, 0.0)
+        mixing[d] = dot(value.astype(bf16), spread) + dot(rest_of(value).astype(bf16), spread)
+    own = window(group * (line_offsets.shape[0] // 4) + block)
+    inverse = repeated(waves, 1) * jnp.concatenate([own] * PARTS, 0)
+    high, low = inverse.astype(bf16), rest_of(inverse).astype(bf16)
+    last[0:64] = high
+    last[64:128] = high
+    last[128:192] = low
+    last[192:256] = low
+
+
+def spectrum_kernel(
+    axes, bins_in, focal_in, lines_in, signal, wide, mixing, last,
+    bins, focal_onsets, line_offsets, held, table, sem, sems,
+):
+    own, focal, samples = held.shape
+    fetches = []
+    for i, (source, target) in enumerate(
+        [(bins_in, bins), (focal_in, focal_onsets), (lines_in, line_offsets)]
+    ):
+        fetches.append(pltpu.make_async_copy(source, target, sems.at[i]))
+        fetches[-1].start()
+    copy = pltpu.make_async_copy(signal, held, sem)
+    copy.start()
+    for fetch in fetches:
+        fetch.wait()
+    waves = waves_of(bins, 8, samples)
+    forward = waves * (1.0 / math.sqrt(samples))
+    table[...] = jnp.concatenate(
+        [repeated(forward, 1), repeated(rest_of(forward), 1)], 0
+    ).T.astype(bf16)
+    fill_tables(axes, waves, bins, focal_onsets, line_offsets, mixing, last)
     both = table[...]
-    for (lo, hi), copy in zip(chunks, copies):
-        copy.wait()
-        x = held[lo:hi].reshape((hi - lo) * focal, samples)
-        rounded = x.astype(bf16)
-        wide[lo * focal : hi * focal] = dot(rounded, both, NT) + dot(
-            (x - rounded.astype(f32)).astype(bf16), both, NT
-        )
+    copy.wait()
+    x = held[...].reshape(own * focal, samples)
+    rounded = x.astype(bf16)
+    wide[...] = dot(rounded, both) + dot((x - rounded.astype(f32)).astype(bf16), both)
 
 
 def pack_kernel(wide, _, out):
@@ -88,48 +131,12 @@
     out[...] = jnp.broadcast_to(packed[None], out.shape)
 
 
-def tables_kernel(axes, bins, focal_onsets, line_offsets, mixing, last):
-    samples = last.shape[1]
-    lines = mixing.shape[2] // LINE
-    block = lax.axis_index(axes[0])
-    group = lax.axis_index(axes[1])
-    forward = waves_of(bins, 8, samples) * (1.0 / math.sqrt(samples))
-    row = iota((FOCAL, samples), 0)
-    time = iota((FOCAL, samples), 1)
-    focal = jnp.zeros((FOCAL, samples), jnp.int32)
-    for f in range(FOCAL):
-        focal = jnp.where(row == f, focal_onsets[f], focal)
-
-    def window(line):
-        onset = focal + line_offsets[line]
-        return jnp.where((time < onset) | (time >= samples - onset), 1.0, 0.0)
-
-    inside = jnp.concatenate([window(block * lines + l) for l in range(lines)], 0)
-    rows = lines * FOCAL
-    count = mixing.shape[2]
-    same = (iota((HALF, rows), 0) & 15) == (iota((HALF, rows), 1) & 15)
-    first = (iota((rows, count), 0) >> 4) * LINE
-    column = iota((rows, count), 1)
-    spread = jnp.where((column >= first) & (column < first + LINE), 1.0, 0.0)
-    for d in range(PARTS):
-        pair = repeated(forward * waves_of(bins, 8, samples, d), 1)
-        value = jnp.where(same, dot(pair, inside, NT, lax.Precision.HIGHEST), 0.0)
-        mixing[d] = dot(value, spread, NN, lax.Precision.HIGHEST)
-    own = window(group * (line_offsets.shape[0] // 4) + block)
-    inverse = repeated(waves_of(bins, 8, samples), 1) * jnp.concatenate([own] * PARTS, 0)
-    high, low = inverse.astype(bf16), rest_of(inverse).astype(bf16)
-    last[0:64] = high
-    last[64:128] = high
-    last[128:192] = low
-    last[192:256] = low
-
-
-def apply_kernel(order, field, kernel, out, high, low, rows, left, sums):
+def apply_kernel(order, field, kernel, out, rows, left, right, sums, tall):
     blocks, half, _ = field.shape
     columns = left.shape[1]
-    count = high.shape[0] // PARTS
+    count = kernel.shape[2]
     spans = [slice(lo, min(lo + SPAN, columns)) for lo in range(0, columns, SPAN)]
-    units = [(span, k) for span in spans for k in range(PARTS)]
+    units = [(span, k) for span in spans for k in (0, 2, 1, 3)]
     ready = [0]
 
     def prepare(span):
@@ -144,34 +151,40 @@
         lane = iota((LANES, LANES), 1)
         for j in range(span.start, span.stop, LANES):
             x = rows[j : j + LANES]
-            left[:, j : j + LANES] = jnp.where(lane < HALF, x, rest_of(x)).T.astype(bf16)
-
-    def split(span, k):
+            x = jnp.where(lane < HALF, x, rest_of(x))
+            right[j : j + LANES] = x.astype(bf16)
+
+    for span in spans:
+        prepare(span)
+        for k in range(PARTS):
+            x = kernel[k // 2, k % 2, :, span]
+            rounded = x.astype(bf16)
+            rest = (x - rounded.astype(f32)).astype(bf16)
+            x = dot(rounded, right[span]) + dot(rest, right[span])
+            tall[k] = x if span.start == 0 else tall[k] + x
+    grown = []
+    for w in range(2):
+        real, imag = tall[2 * w], tall[2 * w + 1]
+        real, imag = real + pltpu.roll(real, HALF, 1), imag + pltpu.roll(imag, HALF, 1)
+        lane = iota(real.shape, 1)
+        crossed = jnp.where(
+            (lane & 16) == 0, -pltpu.roll(imag, LANES - 16, 1), pltpu.roll(imag, 16, 1)
+        )
+        grown.append(real + crossed)
+    out[...] = jnp.where((lane & 32) == 0, grown[0], grown[1]).T[:HALF]
+
+
+def split_kernel(_, kernel, high, low):
+    count, columns = kernel.shape[2:]
+    cut = columns // 256 * LANES
+    for k in range(PARTS):
         for c in range(0, count, 16):
             at = slice(k * count + c, k * count + c + 16)
-            x = kernel[k // 2, k % 2, c : c + 16, span]
-            high[at, span] = x.astype(bf16)
-            x = x - high[at, span].astype(f32)
-            low[at, span] = x.astype(bf16)
-
-    split(*units[0])
-    prepare(spans[0])
-    for i, (span, k) in enumerate(units):
-        at = slice(k * count, (k + 1) * count)
-        w = 32 * (k // 2)
-        upper = left[w : w + 32, span]
-        both = jnp.concatenate([upper, left[HALF + w : HALF + w + 32, span]], 0)
-        x = dot(both, high[at, span], NT)
-        x = x[:32] + x[32:] + dot(upper, low[at, span], NT)
-        sums[k] = x if span.start == 0 else sums[k] + x
-        if i + 1 < len(units):
-            split(*units[i + 1])
-            if units[i + 1][0] is not span:
-                prepare(units[i + 1][0])
-    for w in range(2):
-        real, imag = sums[2 * w], sums[2 * w + 1]
-        out[32 * w : 32 * w + 16] = real[:16] - imag[16:]
-        out[32 * w + 16 : 32 * w + 32] = real[16:] + imag[:16]
+            for span in (slice(0, cut), slice(cut, columns)):
+                x = kernel[k // 2, k % 2, c : c + 16, span]
+                high[at, span] = x.astype(bf16)
+                x = x - high[at, span].astype(f32)
+                low[at, span] = x.astype(bf16)
 
 
 def adjoint_kernel(order, one, other, mixing, high, low, out, flat, rows):
@@ -261,10 +274,8 @@
     waves, _, block_rows, columns = reflectivity.shape
     blocks = columns // own
     half = own // 2
-    lines = block_rows // LINE
     assert (waves, focal, own) == (2, FOCAL, LINE)
     chunks = [(0, 16), (16, 40), (40, 64), (64, own)]
-    early = [(0, 48), (48, own)]
     order = members()
     assert sorted(order) == list(range(blocks))
     exchange = functools.partial(
@@ -278,20 +289,26 @@
     shape = jax.ShapeDtypeStruct
     far = functools.partial(pltpu.with_memory_space_constraint, memory_space=pltpu.HBM)
 
-    wide = call(
-        functools.partial(spectrum_kernel, early),
-        pltpu.VMEM((own * focal, LANES), f32),
-        [ANY, ANY],
-        VMEM,
+    wide, mixing, last = call(
+        functools.partial(spectrum_kernel, ("blk", "cols")),
+        [
+            pltpu.VMEM((own * focal, LANES), f32),
+            pltpu.VMEM((PARTS, HALF, block_rows), f32),
+            pltpu.VMEM((4 * HALF, samples), bf16),
+        ],
+        [ANY] * 4,
+        [VMEM] * 3,
         [
             pltpu.SMEM(frequency_bins.shape, jnp.int32),
+            pltpu.SMEM(focal_onsets.shape, jnp.int32),
+            pltpu.SMEM(line_offsets.shape, jnp.int32),
             pltpu.VMEM((own, focal, samples), f32),
-            pltpu.VMEM((LANES, samples), bf16),
-            pltpu.SemaphoreType.DMA((len(early),)),
+            pltpu.VMEM((samples, LANES), bf16),
             pltpu.SemaphoreType.DMA,
+            pltpu.SemaphoreType.DMA((3,)),
         ],
         limit=16,
-    )(far(frequency_bins), far(focusing_plus))
+    )(far(frequency_bins), far(focal_onsets), far(line_offsets), far(focusing_plus))
     copies = call(
         pack_kernel,
         shape((blocks, half, LANES), f32),
@@ -301,27 +318,29 @@
     )(wide, far(reflectivity))
     field = exchange(copies)
 
-    mixing, last = call(
-        functools.partial(tables_kernel, ("blk", "cols")),
-        [shape((PARTS, HALF, block_rows), f32), shape((4 * HALF, samples), bf16)],
-        [SMEM, SMEM, SMEM],
+    value = call(
+        functools.partial(apply_kernel, order),
+        shape((HALF, block_rows), f32),
         [VMEM, VMEM],
-        cost=1 << 20,
-    )(frequency_bins, focal_onsets, line_offsets)
-
-    value, high, low = call(
-        functools.partial(apply_kernel, order),
-        [shape((HALF, block_rows), f32)] + [pltpu.VMEM((PARTS * block_rows, columns), bf16)] * 2,
-        [VMEM, VMEM],
-        [VMEM] * 3,
+        VMEM,
         [
             pltpu.VMEM((columns, LANES), f32),
             pltpu.VMEM((LANES, columns), bf16),
-            pltpu.VMEM((PARTS, 32, block_rows), f32),
+            pltpu.VMEM((columns, LANES), bf16),
+            pltpu.VMEM((2, 32, block_rows), f32),
+            pltpu.VMEM((4, block_rows, LANES), f32),
         ],
         limit=16,
     )(field, reflectivity)
     value = value + lax.ppermute(value, "cols", [(0, 1), (1, 0), (2, 3), (3, 2)])
+    high, low = call(
+        split_kernel,
+        [pltpu.VMEM((PARTS * block_rows, columns), bf16)] * 2,
+        [ANY, VMEM],
+        [VMEM] * 2,
+        cost=8 << 20,
+        limit=16,
+    )(value, reflectivity)
     other = lax.ppermute(value, "cols", [(0, 2), (2, 0), (1, 3), (3, 1)])
 
     partial_update = call(

time: 57.9 us -> 57.3 us (0.990)
  Pallas kernels: 13.8 us -> 12.2 us
  waiting for transfers between devices: 2.33 us -> 3.39 us
    pallas_call x3, Pallas kernels: 9.22 us -> 7.7 us  [the longest x1 3.79 us: local(): call(functools.partial(apply_kernel, order), shape((HALF, block_rows), f3...]
    ppermute x1, waiting for transfers between devices: 1.04 us -> 2.1 us  [local(): other = lax.ppermute(value, 'cols', [(0, 2), (2, 0), (1, 3), (3, 1)])]
  transfers between devices with their start and end apart: 2 -> 2, of which waited for: 2 -> 2; matrix products, arithmetic and copies ran while one was open for 0% -> 0% of each run, Pallas kernels for 4% -> 2%
where the time goes in v4:
time: 57.3 us; the launch traced here: 57 us
  blocking collectives  38.2 us (67%)
  Pallas kernels  12.2 us (21%)
  waiting for transfers between devices  3.39 us (6%)
  starting transfers between devices  3.05 us (5%)
    all_to_all x1, blocking collectives, local(): field = exchange(copies)  21.4 us
    all_to_all x1, blocking collectives, local(): pieces = exchange(partial_update)  16.8 us
    pallas_call x1, Pallas kernels, local(): call(functools.partial(apply_kernel, order), shape((HALF, block_rows), f3...  3.79 us
    ppermute x1, starting transfers between devices, local(): other = lax.ppermute(value, 'cols', [(0, 2), (2, 0), (1, 3), (3, 1)])  2.98 us
    pallas_call x1, Pallas kernels, local(): call(functools.partial(spectrum_kernel, ('blk', 'cols')), [pltpu.VMEM((ow...  2.56 us
    pallas_call x1, Pallas kernels, local(): call(functools.partial(adjoint_kernel, order), shape((blocks, half, LANES...  2.34 us
    ppermute x1, waiting for transfers between devices, local(): other = lax.ppermute(value, 'cols', [(0, 2), (2, 0), (1, 3), (3, 1)])  2.1 us
    pallas_call x1, Pallas kernels, local(): call(functools.partial(signal_kernel, chunks), shape((own, focal, samples...  1.95 us
  transfers between devices with their start and end apart: 2, of which 2 were waited for; matrix products, arithmetic and copies ran while one was open for 0% of the time, Pallas kernels for 2%

profile of v4, /device:TPU:0, one launch (start us, length us, event | category | flops | bytes accessed | tf_op | source)
XLA Modules:
  0.0 57.0 jit_solution(1231848734879062467)
XLA Ops:
  0.0 2.6 %shard_map.64 = (f32[1216,128]{1,0:T(8,128)S(1)}, f32[4,64,304]{2,1,0:T(8,128)S(1)}, bf16[256,512]{1,0:T(8,128)(2,1)S(1)}) custom-call(s32[2]{0:T(128)} %bins_in.1, s32[16]{0:T(128)} %focal_in.1, s32[128]{0:T(128)} %lines_in.1, f32[76,16,512]{2,1,0:T(8,128)} %signal.1), custom_call_target="tpu_custom_call" | custom-call | tf_op jit(solution)/shard_map/pallas_call | solution.py:292
  2.6 0.0 copy-start
  2.6 0.2 shard_map.65
  2.8 21.4 %all_to_all.10.field = f32[32,38,128]{2,1,0:T(8,128)S(1)} all-to-all(f32[32,38,128]{2,1,0:T(8,128)S(1)} %shard_map.65), channel_id=1, replica_groups={{0,36,72,108,16,52,88,124,32,68,104,12,48,84,120,28,64,100,8,44,80,116,..., dimensions={0} | all-to-all | bytes 1245184 | tf_op jit(solution)/shard_map/all_to_all | solution.py:319
  24.2 0.0 copy-done
  24.2 3.8 %shard_map.66 = f32[64,304]{1,0:T(8,128)S(1)} custom-call(f32[32,38,128]{2,1,0:T(8,128)S(1)} %all_to_all.10.field, f32[2,2,304,2432]{3,2,1,0:T(8,128)S(1)} %copy-done), custom_call_target="tpu_custom_call" | custom-call | tf_op jit(solution)/shard_map/pallas_call | solution.py:321
  28.0 0.1 collective-permute-start
  28.1 1.3 %collective-permute-done = f32[64,304]{1,0:T(8,128)S(1)} collective-permute-done((f32[64,304]{1,0:T(8,128)S(1)}, f32[64,304]{1,0:T(8,128)S(1)}, u32[]{:S(2)}, u32[]{:S(2)}) %collective-permute-start) | collective-permute-done | bytes 77856 | tf_op jit(solution)/shard_map/ppermute | solution.py:335
  29.4 3.0 %collective-permute-start.1 = (f32[64,304]{1,0:T(8,128)S(1)}, f32[64,304]{1,0:T(8,128)S(1)}, u32[]{:S(2)}, u32[]{:S(2)}) collective-permute-start(f32[64,304]{1,0:T(8,128)S(1)} %add.3._.one), channel_id=1, source_target_pairs={{0,2},{2,0},{1,3},{3,1},{4,6},{6,4},{5,7},{7,5},{8,10},{10,8},{9,1... | collective-permute-start | bytes 233480 | tf_op jit(solution)/shard_map/ppermute | solution.py:344
  32.4 1.4 %shard_map.67 = (bf16[1216,2432]{1,0:T(8,128)(2,1)S(1)}, bf16[1216,2432]{1,0:T(8,128)(2,1)S(1)}) custom-call(f32[64,304]{1,0:T(8,128)S(1)} %add.3._.one, f32[2,2,304,2432]{3,2,1,0:T(8,128)S(1)} %copy-done), custom_call_target="tpu_custom_call" | custom-call | flops 8388608 | bytes 8388608 | tf_op jit(solution)/shard_map/pallas_call | solution.py:336
  33.7 2.1 %collective-permute-done.1.other = f32[64,304]{1,0:T(8,128)S(1)} collective-permute-done((f32[64,304]{1,0:T(8,128)S(1)}, f32[64,304]{1,0:T(8,128)S(1)}, u32[]{:S(2)}, u32[]{:S(2)}) %collective-permute-start.1) | collective-permute-done | bytes 77856 | tf_op jit(solution)/shard_map/ppermute | solution.py:344
  35.8 0.0 copy-start.1
  35.8 2.3 %shard_map.68 = f32[32,38,128]{2,1,0:T(8,128)S(1)} custom-call(f32[64,304]{1,0:T(8,128)S(1)} %add.3._.one, f32[64,304]{1,0:T(8,128)S(1)} %collective-permute-done.1.other, f32[4,64,304]{2,1,0:T(8,128)S(1)} %get-tuple-element.11.mixing, bf16[1216,2432]{1,0:T(8,128)(2,1)S(1)} %get-tuple-element.12.high, bf16[1216,2432]{1,0:T(8,128)(2,1)S(1)} %get-tuple-element.13.low), custom_call_target="tpu_custom_call" | custom-call | tf_op jit(solution)/shard_map/pallas_call | solution.py:346
  38.2 16.8 %all_to_all.11.pieces = f32[32,38,128]{2,1,0:T(8,128)S(1)} all-to-all(f32[32,38,128]{2,1,0:T(8,128)S(1)} %shard_map.68), channel_id=1, replica_groups={{0,36,72,108,16,52,88,124,32,68,104,12,48,84,120,28,64,100,8,44,80,116,..., dimensions={0} | all-to-all | bytes 1245184 | tf_op jit(solution)/shard_map/all_to_all | solution.py:353
  55.0 0.0 copy-done.1
  55.0 2.0 %shard_map.69 = f32[76,16,512]{2,1,0:T(8,128)} custom-call(f32[32,38,128]{2,1,0:T(8,128)S(1)} %all_to_all.11.pieces, bf16[256,512]{1,0:T(8,128)(2,1)S(1)} %get-tuple-element.14.last, f32[76,16,512]{2,1,0:T(8,128)S(1)} %copy-done.1), custom_call_target="tpu_custom_call" | custom-call | tf_op jit(solution)/shard_map/pallas_call | solution.py:355
  (1 shorter events, 0.0 us)
Async XLA Ops:
  2.6 21.7 %copy-start = (f32[2,2,304,2432]{3,2,1,0:T(8,128)S(1)}, f32[2,2,304,2432]{3,2,1,0:T(8,128)}, u32[]{:S(2)}) copy-start(f32[2,2,304,2432]{3,2,1,0:T(8,128)} %kernel.3) | copy-start | bytes 35487748
  28.0 1.4 %collective-permute-start = (f32[64,304]{1,0:T(8,128)S(1)}, f32[64,304]{1,0:T(8,128)S(1)}, u32[]{:S(2)}, u32[]{:S(2)}) collective-permute-start(f32[64,304]{1,0:T(8,128)S(1)} %shard_map.66), channel_id=1, source_target_pairs={{0,1},{1,0},{2,3},{3,2},{4,5},{5,4},{6,7},{7,6},{8,9},{9,8},{10,11... | collective-permute-start | bytes 233480 | tf_op jit(solution)/shard_map/ppermute | solution.py:335
  29.4 6.4 %collective-permute-start.1 = (f32[64,304]{1,0:T(8,128)S(1)}, f32[64,304]{1,0:T(8,128)S(1)}, u32[]{:S(2)}, u32[]{:S(2)}) collective-permute-start(f32[64,304]{1,0:T(8,128)S(1)} %add.3._.one), channel_id=1, source_target_pairs={{0,2},{2,0},{1,3},{3,1},{4,6},{6,4},{5,7},{7,5},{8,10},{10,8},{9,1... | collective-permute-start | bytes 233480 | tf_op jit(solution)/shard_map/ppermute | solution.py:344
  35.8 19.2 %copy-start.1 = (f32[76,16,512]{2,1,0:T(8,128)S(1)}, f32[76,16,512]{2,1,0:T(8,128)}, u32[]{:S(2)}) copy-start(f32[76,16,512]{2,1,0:T(8,128)} %direct.1) | copy-start | bytes 7471108

commit v5 on v4

--- a/solution.py
+++ b/solution.py
@@ -171,7 +171,9 @@
             (lane & 16) == 0, -pltpu.roll(imag, LANES - 16, 1), pltpu.roll(imag, 16, 1)
         )
         grown.append(real + crossed)
-    out[...] = jnp.where((lane & 32) == 0, grown[0], grown[1]).T[:HALF]
+    value = jnp.where((lane & 32) == 0, grown[0], grown[1])
+    short = out.shape[0]
+    out[...] = jnp.where(lane[:short] < HALF, value[:short], value[short:])
 
 
 def split_kernel(_, kernel, high, low):
@@ -190,6 +192,10 @@
 def adjoint_kernel(order, one, other, mixing, high, low, out, flat, rows):
     count = high.shape[0] // PARTS
     x = one[...] + other[...]
+    turned = pltpu.roll(x, HALF, 1)
+    low_half = iota(x.shape, 1) < HALF
+    x = jnp.concatenate([jnp.where(low_half, x, turned), jnp.where(low_half, turned, x)], 0)
+    x = x.T[:HALF]
     minus = mixing[0] * x
     for d in range(1, PARTS):
         at = FOCAL * d
@@ -320,7 +326,7 @@
 
     value = call(
         functools.partial(apply_kernel, order),
-        shape((HALF, block_rows), f32),
+        shape((block_rows // 2, LANES), f32),
         [VMEM, VMEM],
         VMEM,
         [

time: 57.3 us -> 57.1 us (level)
  no operation moved by 1% of the time
where the time goes in v5:
time: 57.1 us; the launch traced here: 56.7 us
  blocking collectives  38.2 us (67%)
  Pallas kernels  12.4 us (22%)
  starting transfers between devices  3.07 us (5%)
  waiting for transfers between devices  2.92 us (5%)
    all_to_all x1, blocking collectives, local(): field = exchange(copies)  21.4 us
    all_to_all x1, blocking collectives, local(): pieces = exchange(partial_update)  16.8 us
    pallas_call x1, Pallas kernels, local(): call(functools.partial(apply_kernel, order), shape((block_rows // 2, LANE...  3.77 us
    ppermute x1, starting transfers between devices, local(): other = lax.ppermute(value, 'cols', [(0, 2), (2, 0), (1, 3), (3, 1)])  2.99 us
    pallas_call x1, Pallas kernels, local(): call(functools.partial(spectrum_kernel, ('blk', 'cols')), [pltpu.VMEM((ow...  2.56 us
    pallas_call x1, Pallas kernels, local(): call(functools.partial(adjoint_kernel, order), shape((blocks, half, LANES...  2.53 us
    pallas_call x1, Pallas kernels, local(): call(functools.partial(signal_kernel, chunks), shape((own, focal, samples...  1.96 us
    ppermute x1, waiting for transfers between devices, local(): other = lax.ppermute(value, 'cols', [(0, 2), (2, 0), (1, 3), (3, 1)])  1.66 us
  transfers between devices with their start and end apart: 2, of which 2 were waited for; matrix products, arithmetic and copies ran while one was open for 0% of the time, Pallas kernels for 2%

profile of v5, /device:TPU:0, one launch (start us, length us, event | category | flops | bytes accessed | tf_op | source)
XLA Modules:
  0.0 56.7 jit_solution(6776289804272363168)
XLA Ops:
  0.0 2.6 %shard_map.64 = (f32[1216,128]{1,0:T(8,128)S(1)}, f32[4,64,304]{2,1,0:T(8,128)S(1)}, bf16[256,512]{1,0:T(8,128)(2,1)S(1)}) custom-call(s32[2]{0:T(128)} %bins_in.1, s32[16]{0:T(128)} %focal_in.1, s32[128]{0:T(128)} %lines_in.1, f32[76,16,512]{2,1,0:T(8,128)} %signal.1), custom_call_target="tpu_custom_call" | custom-call | tf_op jit(solution)/shard_map/pallas_call | solution.py:298
  2.6 0.0 copy-start
  2.6 0.2 shard_map.65
  2.8 21.4 %all_to_all.10.field = f32[32,38,128]{2,1,0:T(8,128)S(1)} all-to-all(f32[32,38,128]{2,1,0:T(8,128)S(1)} %shard_map.65), channel_id=1, replica_groups={{0,36,72,108,16,52,88,124,32,68,104,12,48,84,120,28,64,100,8,44,80,116,..., dimensions={0} | all-to-all | bytes 1245184 | tf_op jit(solution)/shard_map/all_to_all | solution.py:325
  24.2 0.0 copy-done
  24.2 3.8 %shard_map.66 = f32[152,128]{1,0:T(8,128)S(1)} custom-call(f32[32,38,128]{2,1,0:T(8,128)S(1)} %all_to_all.10.field, f32[2,2,304,2432]{3,2,1,0:T(8,128)S(1)} %copy-done), custom_call_target="tpu_custom_call" | custom-call | tf_op jit(solution)/shard_map/pallas_call | solution.py:327
  28.0 0.1 collective-permute-start
  28.1 1.3 %collective-permute-done = f32[152,128]{1,0:T(8,128)S(1)} collective-permute-done((f32[152,128]{1,0:T(8,128)S(1)}, f32[152,128]{1,0:T(8,128)S(1)}, u32[]{:S(2)}, u32[]{:S(2)}) %collective-permute-start) | collective-permute-done | bytes 77856 | tf_op jit(solution)/shard_map/ppermute | solution.py:341
  29.4 3.0 %collective-permute-start.1 = (f32[152,128]{1,0:T(8,128)S(1)}, f32[152,128]{1,0:T(8,128)S(1)}, u32[]{:S(2)}, u32[]{:S(2)}) collective-permute-start(f32[152,128]{1,0:T(8,128)S(1)} %add.3._.one), channel_id=1, source_target_pairs={{0,2},{2,0},{1,3},{3,1},{4,6},{6,4},{5,7},{7,5},{8,10},{10,8},{9,1... | collective-permute-start | bytes 233480 | tf_op jit(solution)/shard_map/ppermute | solution.py:350
  32.4 1.4 %shard_map.67 = (bf16[1216,2432]{1,0:T(8,128)(2,1)S(1)}, bf16[1216,2432]{1,0:T(8,128)(2,1)S(1)}) custom-call(f32[152,128]{1,0:T(8,128)S(1)} %add.3._.one, f32[2,2,304,2432]{3,2,1,0:T(8,128)S(1)} %copy-done), custom_call_target="tpu_custom_call" | custom-call | flops 8388608 | bytes 8388608 | tf_op jit(solution)/shard_map/pallas_call | solution.py:342
  33.7 1.7 %collective-permute-done.1.other = f32[152,128]{1,0:T(8,128)S(1)} collective-permute-done((f32[152,128]{1,0:T(8,128)S(1)}, f32[152,128]{1,0:T(8,128)S(1)}, u32[]{:S(2)}, u32[]{:S(2)}) %collective-permute-start.1) | collective-permute-done | bytes 77856 | tf_op jit(solution)/shard_map/ppermute | solution.py:350
  35.4 0.0 copy-start.1
  35.4 2.5 %shard_map.68 = f32[32,38,128]{2,1,0:T(8,128)S(1)} custom-call(f32[152,128]{1,0:T(8,128)S(1)} %add.3._.one, f32[152,128]{1,0:T(8,128)S(1)} %collective-permute-done.1.other, f32[4,64,304]{2,1,0:T(8,128)S(1)} %get-tuple-element.11.mixing, bf16[1216,2432]{1,0:T(8,128)(2,1)S(1)} %get-tuple-element.12.high, bf16[1216,2432]{1,0:T(8,128)(2,1)S(1)} %get-tuple-element.13.low), custom_call_target="tpu_custom_call" | custom-call | tf_op jit(solution)/shard_map/pallas_call | solution.py:352
  37.9 16.8 %all_to_all.11.pieces = f32[32,38,128]{2,1,0:T(8,128)S(1)} all-to-all(f32[32,38,128]{2,1,0:T(8,128)S(1)} %shard_map.68), channel_id=1, replica_groups={{0,36,72,108,16,52,88,124,32,68,104,12,48,84,120,28,64,100,8,44,80,116,..., dimensions={0} | all-to-all | bytes 1245184 | tf_op jit(solution)/shard_map/all_to_all | solution.py:359
  54.7 0.0 copy-done.1
  54.7 2.0 %shard_map.69 = f32[76,16,512]{2,1,0:T(8,128)} custom-call(f32[32,38,128]{2,1,0:T(8,128)S(1)} %all_to_all.11.pieces, bf16[256,512]{1,0:T(8,128)(2,1)S(1)} %get-tuple-element.14.last, f32[76,16,512]{2,1,0:T(8,128)S(1)} %copy-done.1), custom_call_target="tpu_custom_call" | custom-call | tf_op jit(solution)/shard_map/pallas_call | solution.py:361
  (1 shorter events, 0.0 us)
Async XLA Ops:
  2.6 21.7 %copy-start = (f32[2,2,304,2432]{3,2,1,0:T(8,128)S(1)}, f32[2,2,304,2432]{3,2,1,0:T(8,128)}, u32[]{:S(2)}) copy-start(f32[2,2,304,2432]{3,2,1,0:T(8,128)} %kernel.3) | copy-start | bytes 35487748
  28.0 1.4 %collective-permute-start = (f32[152,128]{1,0:T(8,128)S(1)}, f32[152,128]{1,0:T(8,128)S(1)}, u32[]{:S(2)}, u32[]{:S(2)}) collective-permute-start(f32[152,128]{1,0:T(8,128)S(1)} %shard_map.66), channel_id=1, source_target_pairs={{0,1},{1,0},{2,3},{3,2},{4,5},{5,4},{6,7},{7,6},{8,9},{9,8},{10,11... | collective-permute-start | bytes 233480 | tf_op jit(solution)/shard_map/ppermute | solution.py:341
  29.4 6.0 %collective-permute-start.1 = (f32[152,128]{1,0:T(8,128)S(1)}, f32[152,128]{1,0:T(8,128)S(1)}, u32[]{:S(2)}, u32[]{:S(2)}) collective-permute-start(f32[152,128]{1,0:T(8,128)S(1)} %add.3._.one), channel_id=1, source_target_pairs={{0,2},{2,0},{1,3},{3,1},{4,6},{6,4},{5,7},{7,5},{8,10},{10,8},{9,1... | collective-permute-start | bytes 233480 | tf_op jit(solution)/shard_map/ppermute | solution.py:350
  35.4 19.4 %copy-start.1 = (f32[76,16,512]{2,1,0:T(8,128)S(1)}, f32[76,16,512]{2,1,0:T(8,128)}, u32[]{:S(2)}) copy-start(f32[76,16,512]{2,1,0:T(8,128)} %direct.1) | copy-start | bytes 7471108

commit v6 on v5

--- a/solution.py
+++ b/solution.py
@@ -281,7 +281,7 @@
     blocks = columns // own
     half = own // 2
     assert (waves, focal, own) == (2, FOCAL, LINE)
-    chunks = [(0, 16), (16, 40), (40, 64), (64, own)]
+    chunks = [(0, 16), (16, 44), (44, own)]
     order = members()
     assert sorted(order) == list(range(blocks))
     exchange = functools.partial(

time: 57.1 us -> 57.1 us (level)
  no operation moved by 1% of the time
where the time goes in v6:
time: 57.1 us; the launch traced here: 56.7 us
  blocking collectives  38.2 us (67%)
  Pallas kernels  12.4 us (22%)
  starting transfers between devices  3.07 us (5%)
  waiting for transfers between devices  2.92 us (5%)
    all_to_all x1, blocking collectives, local(): field = exchange(copies)  21.4 us
    all_to_all x1, blocking collectives, local(): pieces = exchange(partial_update)  16.8 us
    pallas_call x1, Pallas kernels, local(): call(functools.partial(apply_kernel, order), shape((block_rows // 2, LANE...  3.77 us
    ppermute x1, starting transfers between devices, local(): other = lax.ppermute(value, 'cols', [(0, 2), (2, 0), (1, 3), (3, 1)])  2.99 us
    pallas_call x1, Pallas kernels, local(): call(functools.partial(spectrum_kernel, ('blk', 'cols')), [pltpu.VMEM((ow...  2.56 us
    pallas_call x1, Pallas kernels, local(): call(functools.partial(adjoint_kernel, order), shape((blocks, half, LANES...  2.53 us
    pallas_call x1, Pallas kernels, local(): call(functools.partial(signal_kernel, chunks), shape((own, focal, samples...  1.96 us
    ppermute x1, waiting for transfers between devices, local(): other = lax.ppermute(value, 'cols', [(0, 2), (2, 0), (1, 3), (3, 1)])  1.66 us
  transfers between devices with their start and end apart: 2, of which 2 were waited for; matrix products, arithmetic and copies ran while one was open for 0% of the time, Pallas kernels for 2%

profile of v6, /device:TPU:0, one launch (start us, length us, event | category | flops | bytes accessed | tf_op | source)
XLA Modules:
  0.0 56.7 jit_solution(7451770066627618625)
XLA Ops:
  0.0 2.6 %shard_map.64 = (f32[1216,128]{1,0:T(8,128)S(1)}, f32[4,64,304]{2,1,0:T(8,128)S(1)}, bf16[256,512]{1,0:T(8,128)(2,1)S(1)}) custom-call(s32[2]{0:T(128)} %bins_in.1, s32[16]{0:T(128)} %focal_in.1, s32[128]{0:T(128)} %lines_in.1, f32[76,16,512]{2,1,0:T(8,128)} %signal.1), custom_call_target="tpu_custom_call" | custom-call | tf_op jit(solution)/shard_map/pallas_call | solution.py:298
  2.6 0.0 copy-start
  2.6 0.2 shard_map.65
  2.8 21.4 %all_to_all.10.field = f32[32,38,128]{2,1,0:T(8,128)S(1)} all-to-all(f32[32,38,128]{2,1,0:T(8,128)S(1)} %shard_map.65), channel_id=1, replica_groups={{0,36,72,108,16,52,88,124,32,68,104,12,48,84,120,28,64,100,8,44,80,116,..., dimensions={0} | all-to-all | bytes 1245184 | tf_op jit(solution)/shard_map/all_to_all | solution.py:325
  24.2 0.0 copy-done
  24.2 3.8 %shard_map.66 = f32[152,128]{1,0:T(8,128)S(1)} custom-call(f32[32,38,128]{2,1,0:T(8,128)S(1)} %all_to_all.10.field, f32[2,2,304,2432]{3,2,1,0:T(8,128)S(1)} %copy-done), custom_call_target="tpu_custom_call" | custom-call | tf_op jit(solution)/shard_map/pallas_call | solution.py:327
  28.0 0.1 collective-permute-start
  28.1 1.3 %collective-permute-done = f32[152,128]{1,0:T(8,128)S(1)} collective-permute-done((f32[152,128]{1,0:T(8,128)S(1)}, f32[152,128]{1,0:T(8,128)S(1)}, u32[]{:S(2)}, u32[]{:S(2)}) %collective-permute-start) | collective-permute-done | bytes 77856 | tf_op jit(solution)/shard_map/ppermute | solution.py:341
  29.4 3.0 %collective-permute-start.1 = (f32[152,128]{1,0:T(8,128)S(1)}, f32[152,128]{1,0:T(8,128)S(1)}, u32[]{:S(2)}, u32[]{:S(2)}) collective-permute-start(f32[152,128]{1,0:T(8,128)S(1)} %add.3._.one), channel_id=1, source_target_pairs={{0,2},{2,0},{1,3},{3,1},{4,6},{6,4},{5,7},{7,5},{8,10},{10,8},{9,1... | collective-permute-start | bytes 233480 | tf_op jit(solution)/shard_map/ppermute | solution.py:350
  32.4 1.4 %shard_map.67 = (bf16[1216,2432]{1,0:T(8,128)(2,1)S(1)}, bf16[1216,2432]{1,0:T(8,128)(2,1)S(1)}) custom-call(f32[152,128]{1,0:T(8,128)S(1)} %add.3._.one, f32[2,2,304,2432]{3,2,1,0:T(8,128)S(1)} %copy-done), custom_call_target="tpu_custom_call" | custom-call | flops 8388608 | bytes 8388608 | tf_op jit(solution)/shard_map/pallas_call | solution.py:342
  33.7 1.7 %collective-permute-done.1.other = f32[152,128]{1,0:T(8,128)S(1)} collective-permute-done((f32[152,128]{1,0:T(8,128)S(1)}, f32[152,128]{1,0:T(8,128)S(1)}, u32[]{:S(2)}, u32[]{:S(2)}) %collective-permute-start.1) | collective-permute-done | bytes 77856 | tf_op jit(solution)/shard_map/ppermute | solution.py:350
  35.4 0.0 copy-start.1
  35.4 2.5 %shard_map.68 = f32[32,38,128]{2,1,0:T(8,128)S(1)} custom-call(f32[152,128]{1,0:T(8,128)S(1)} %add.3._.one, f32[152,128]{1,0:T(8,128)S(1)} %collective-permute-done.1.other, f32[4,64,304]{2,1,0:T(8,128)S(1)} %get-tuple-element.11.mixing, bf16[1216,2432]{1,0:T(8,128)(2,1)S(1)} %get-tuple-element.12.high, bf16[1216,2432]{1,0:T(8,128)(2,1)S(1)} %get-tuple-element.13.low), custom_call_target="tpu_custom_call" | custom-call | tf_op jit(solution)/shard_map/pallas_call | solution.py:352
  37.9 16.8 %all_to_all.11.pieces = f32[32,38,128]{2,1,0:T(8,128)S(1)} all-to-all(f32[32,38,128]{2,1,0:T(8,128)S(1)} %shard_map.68), channel_id=1, replica_groups={{0,36,72,108,16,52,88,124,32,68,104,12,48,84,120,28,64,100,8,44,80,116,..., dimensions={0} | all-to-all | bytes 1245184 | tf_op jit(solution)/shard_map/all_to_all | solution.py:359
  54.7 0.0 copy-done.1
  54.7 2.0 %shard_map.69 = f32[76,16,512]{2,1,0:T(8,128)} custom-call(f32[32,38,128]{2,1,0:T(8,128)S(1)} %all_to_all.11.pieces, bf16[256,512]{1,0:T(8,128)(2,1)S(1)} %get-tuple-element.14.last, f32[76,16,512]{2,1,0:T(8,128)S(1)} %copy-done.1), custom_call_target="tpu_custom_call" | custom-call | tf_op jit(solution)/shard_map/pallas_call | solution.py:361
  (1 shorter events, 0.0 us)
Async XLA Ops:
  2.6 21.7 %copy-start = (f32[2,2,304,2432]{3,2,1,0:T(8,128)S(1)}, f32[2,2,304,2432]{3,2,1,0:T(8,128)}, u32[]{:S(2)}) copy-start(f32[2,2,304,2432]{3,2,1,0:T(8,128)} %kernel.3) | copy-start | bytes 35487748
  28.0 1.4 %collective-permute-start = (f32[152,128]{1,0:T(8,128)S(1)}, f32[152,128]{1,0:T(8,128)S(1)}, u32[]{:S(2)}, u32[]{:S(2)}) collective-permute-start(f32[152,128]{1,0:T(8,128)S(1)} %shard_map.66), channel_id=1, source_target_pairs={{0,1},{1,0},{2,3},{3,2},{4,5},{5,4},{6,7},{7,6},{8,9},{9,8},{10,11... | collective-permute-start | bytes 233480 | tf_op jit(solution)/shard_map/ppermute | solution.py:341
  29.4 6.0 %collective-permute-start.1 = (f32[152,128]{1,0:T(8,128)S(1)}, f32[152,128]{1,0:T(8,128)S(1)}, u32[]{:S(2)}, u32[]{:S(2)}) collective-permute-start(f32[152,128]{1,0:T(8,128)S(1)} %add.3._.one), channel_id=1, source_target_pairs={{0,2},{2,0},{1,3},{3,1},{4,6},{6,4},{5,7},{7,5},{8,10},{10,8},{9,1... | collective-permute-start | bytes 233480 | tf_op jit(solution)/shard_map/ppermute | solution.py:350
  35.4 19.4 %copy-start.1 = (f32[76,16,512]{2,1,0:T(8,128)S(1)}, f32[76,16,512]{2,1,0:T(8,128)}, u32[]{:S(2)}) copy-start(f32[76,16,512]{2,1,0:T(8,128)} %direct.1) | copy-start | bytes 7471108
